TPU v7x, 256 devices: a whole 4x4x8 slice. The times are simulated.
256 devices in a mesh: fold: 8 (over x, core), dom: 32 (over z, y).
Axes of the slice: x: 4, y: 4, z: 8, core: 2. Of those that a mesh axis runs over, the one named last changes fastest.
Arguments:
- iterate: float32 [176, 8, 65536], P(None, 'fold', 'dom'), may hold values from -6 to 6
- right_side: float32 [176, 8, 65536], P(None, 'fold', 'dom'), may hold values from -6 to 6
- jacobian: float32 [8, 65536], P('fold', 'dom'), may hold values from 0.5 to 2
- face_scale: float32 [4, 8, 65536], P(None, 'fold', 'dom'), may hold values from 0.3 to 1.5
- face_offset: int32 [4, 8, 65536], P(None, 'fold', 'dom'), may hold values from -512 to 512, as said below
- agglomerate: int32 [8, 65536], P('fold', 'dom'), may hold values from 0 to 255, as said below
- live_count: int32 [8, 32], P('fold', 'dom'), may hold values from 819 to 2048, as said below
- stiff_fine: float32 [176, 176], replicated, as said below
- flux_fine: float32 [4, 176, 176], replicated, may hold values from -0.4375 to 0.4375
- smoother: float32 [176, 176], replicated
- restrict_mid: float32 [56, 176], replicated, may hold values from -0.4375 to 0.4375
- restrict_low: float32 [24, 56], replicated, may hold values from -0.75 to 0.75
Outputs:
- updated: float32 [176, 8, 65536], P(None, 'fold', 'dom')
- residual: float32 [176, 8, 65536], P(None, 'fold', 'dom')
Inputs may be any that keep to these rules, and one draw needn't show every extreme that they name: `face_offset`: 0 marks a wall face; an offset that leads outside its fold plane also acts as a wall; offsets of +512 and -512 occur. `agglomerate`: coarse slots are local to the device of the element. `live_count`: the elements of a device fill its first slots; some device is full. `stiff_fine`: symmetric.
All inputs are finite; a program needn't handle non-finite values.
Results may differ from a plain program's by a relative error of at most 0.0003.
Values sent between devices are 32-bit elements; how exact they have to be, the bound alone decides.
A program may use at most 128 MiB of HBM per device.

v0:
```python
from functools import partial

import jax
import jax.numpy as jnp
from jax import lax
from jax.sharding import PartitionSpec as P

AGG = 8
HLEV = 2
HALO = 512
EC_DEV = 256


PRECISE = lax.Precision.HIGHEST
DAMPING = 0.8


def padded(value, sides, width):
    for axis, dim in sides:
        count, length = (lax.axis_size(axis), value.shape[dim])
        up = [(i, (i + 1) % count) for i in range(count - 1)]
        down = [(j, i) for i, j in up]
        last = lax.slice_in_dim(value, length - width, length, axis=dim)
        first = lax.slice_in_dim(value, 0, width, axis=dim)
        before = lax.ppermute(last, axis, up)
        after = lax.ppermute(first, axis, down)
        value = jnp.concatenate([before, value, after], axis=dim)
    return value


def swapped(block, axis, distance):
    count = lax.axis_size(axis)
    route = []
    for low in range(count):
        high = low | 1 << distance
        if high != low and high < count:
            route += [(low, high), (high, low)]
    return lax.ppermute(block, axis, route)


def product(former, latter):
    return jnp.dot(former, latter, precision=PRECISE, preferred_element_type=jnp.float32)


def galerkin(restrict, matrix):
    return product(product(restrict, matrix), restrict.T)


def galerkin_all(restrict, fluxes):
    return jax.vmap(partial(galerkin, restrict))(fluxes)


def face_sum(extended, offset, offset_rows, scale_rows, fluxes, columns):
    target = jnp.arange(columns, dtype=jnp.int32)[None, :] + offset + offset_rows
    picked = jnp.take(extended, target, axis=1)
    weights = jnp.where(offset_rows != 0, scale_rows, jnp.zeros_like(scale_rows))
    return jnp.einsum("fab,bfn->an", fluxes, picked * weights[None], precision=PRECISE)


def fine_apply(vector, jac_row, scale_rows, offset_rows, active, stiffness, fluxes):
    extended = padded(vector, (("dom", 1),), HALO)
    coupled = face_sum(extended, HALO, offset_rows, scale_rows, fluxes, vector.shape[1])
    return active * (jac_row * product(stiffness, vector) + coupled)


def level_apply(vector, jac_row, scale_rows, offset_rows, active, stiffness, fluxes):
    extended = padded(vector, (("dom", 1),), HALO)
    coupled = face_sum(extended, HALO, offset_rows, scale_rows, fluxes, vector.shape[1])
    return active * (jac_row * product(stiffness, vector) + coupled)


def on_device(
    iterate,
    right_side,
    jacobian,
    face_scale,
    face_offset,
    agglomerate,
    live_count,
    stiff_fine,
    flux_fine,
    smoother,
    restrict_mid,
    restrict_low,
):
    columns = iterate.shape[2]
    vec_iter = iterate[:, 0, :]
    vec_rhs = right_side[:, 0, :]
    scale_rows = face_scale[:, 0, :]
    offset_rows = face_offset[:, 0, :]
    active = (jnp.arange(columns, dtype=jnp.int32)[None, :] < live_count[0, 0]).astype(jnp.float32)
    stiff_mid = galerkin(restrict_mid, stiff_fine)
    flux_mid = galerkin_all(restrict_mid, flux_fine)
    stiff_low = galerkin(restrict_low, stiff_mid)
    flux_low = galerkin_all(restrict_low, flux_mid)
    diag_mid = jnp.diagonal(stiff_mid)[:, None]
    diag_low = jnp.diagonal(stiff_low)[:, None]
    masked = active * vec_iter
    target_side = active * vec_rhs
    first_res = target_side - fine_apply(
        masked, jacobian, scale_rows, offset_rows, active, stiff_fine, flux_fine
    )
    smoothed = masked + active * product(smoother, first_res) / jacobian
    second = target_side - fine_apply(
        smoothed, jacobian, scale_rows, offset_rows, active, stiff_fine, flux_fine
    )
    mid_rhs = product(restrict_mid, second)
    mid_corr = DAMPING * active * mid_rhs / (jacobian * diag_mid)
    mid_res = mid_rhs - level_apply(
        mid_corr, jacobian, scale_rows, offset_rows, active, stiff_mid, flux_mid
    )
    low_rhs = product(restrict_low, mid_res)
    low_corr = DAMPING * active * low_rhs / (jacobian * diag_low)
    low_res = low_rhs - level_apply(
        low_corr, jacobian, scale_rows, offset_rows, active, stiff_low, flux_low
    )
    onehot = (agglomerate[0][:, None] == jnp.arange(EC_DEV, dtype=jnp.int32)[None, :]).astype(
        jnp.float32
    )
    coarse = product(low_res, onehot)
    sections = []
    for height in range(HLEV):
        factor = AGG * 2**height
        sections.append(DAMPING * coarse / (factor * diag_low))
        residue = coarse - DAMPING * product(stiff_low, coarse / diag_low)
        arrived = swapped(residue, "fold", height)
        coarse = residue + arrived
    coarse_corr = DAMPING * coarse / (AGG * 2**HLEV * diag_low)
    for height in reversed(range(HLEV)):
        coarse_corr = sections[height] + coarse_corr
    low_total = low_corr + active * product(coarse_corr, onehot.T)
    mid_total = mid_corr + product(restrict_low.T, low_total)
    updated = smoothed + product(restrict_mid.T, mid_total)
    lifted_stiff = product(stiff_fine, restrict_mid.T)
    lifted_flux = jax.vmap(lambda block: product(block, restrict_mid.T))(flux_fine)
    mid_extended = padded(mid_total, (("dom", 1),), HALO)
    lifted_coupled = face_sum(mid_extended, HALO, offset_rows, scale_rows, lifted_flux, columns)
    residual = second - active * (jacobian * product(lifted_stiff, mid_total) + lifted_coupled)
    return (updated[:, None, :], residual[:, None, :])


def solution(mesh):
    return jax.shard_map(
        on_device,
        mesh=mesh,
        in_specs=(
            P(None, "fold", "dom"),
            P(None, "fold", "dom"),
            P("fold", "dom"),
            P(None, "fold", "dom"),
            P(None, "fold", "dom"),
            P("fold", "dom"),
            P("fold", "dom"),
            P(),
            P(),
            P(),
            P(),
            P(),
        ),
        out_specs=(P(None, "fold", "dom"), P(None, "fold", "dom")),
        check_vma=False,
    )
```

profile of v0, /device:TPU:124, one launch (start us, length us, event | category | flops | bytes accessed | tf_op | source)
XLA Modules:
  0.0 311.5 jit_solution(9310839136433368300)
XLA Ops:
  1.4 1.9 bitcast_multiply_fusion.13
  3.3 0.9 fusion.98
  4.2 4.8 %collective-permute-start = (f32[176,512]{1,0:T(8,128)}, f32[176,512]{1,0:T(8,128)S(1)}, u32[]{:S(2)}, u32[]{:S(2)}) collective-permute-start(f32[176,512]{1,0:T(8,128)} %get-tuple-element.10), channel_id=1, source_target_pairs={{0,1},{1,2},{2,3},{3,4},{4,5},{5,6},{6,7},{7,8},{8,9},{9,10},{10,1... | collective-permute-start | bytes 1081352 | tf_op jit(solution)/shard_map/ppermute | solution.py:25
  9.1 1.9 collective-permute-start.1
  11.1 0.6 fusion.63
  11.6 1.6 fusion.60
  14.1 1.0 gather_fusion
  15.5 0.4 convolution_bitcast_fusion.6
  15.9 0.8 gather_fusion.1
  17.0 7.4 %collective-permute-done.1 = f32[176,512]{1,0:T(8,128)} collective-permute-done((f32[176,512]{1,0:T(8,128)}, f32[176,512]{1,0:T(8,128)}, u32[]{:S(2)}, u32[]{:S(2)}) %collective-permute-start.1) | collective-permute-done | bytes 360480 | tf_op jit(solution)/shard_map/ppermute | solution.py:26
  24.5 2.6 pad_maximum_fusion
  27.1 3.3 %copy.25 = f32[176,3072]{0,1:T(8,128)} copy(f32[176,3072]{1,0:T(8,128)} %pad_maximum_fusion) | data formatting | bytes 4325376 | tf_op jit(solution)/shard_map/concatenate | solution.py:27
  30.4 33.2 %gather_fusion.3 = f32[8192,176]{1,0:T(8,128)} fusion(f32[176,3072]{0,1:T(8,128)} %copy.25, s32[8192]{0:T(1024)S(1)} %broadcast_clamp_fusion.1), kind=kCustom, calls=%fused_computation.clone | custom fusion | bytes 11567104 | tf_op jit(solution)/shard_map/jit(_take)/gather | solution.py:55
  63.6 8.3 %copy.26 = f32[4,2048,176]{1,2,0:T(8,128)} copy(f32[4,2048,176]{2,1,0:T(8,128)} %bitcast.165) | data formatting | bytes 11534336 | tf_op jit(solution)/shard_map/jit(_take)/gather | solution.py:55
  71.9 6.9 %fusion.31 = f32[2048,176]{0,1:T(8,128)S(1)} fusion(f32[4,176,176]{2,1,0:T(8,128)S(1)} %copy-done, f32[4,2048,176]{1,2,0:T(8,128)} %copy.26, f32[4,2048]{1,0:T(4,128)S(1)} %bitcast_select_fusion, pred[4,2048]{1,0:T(4,128)(4,1)S(1)} %compare_and_fusion), kind=kOutput, calls=%fused_computation.45 | convolution fusion | flops 3047948288 | bytes 7745536 | tf_op jit(solution)/shard_map/fab,bfn->an/dot_general | solution.py:57
  78.9 2.3 fusion.21
  81.2 1.9 fusion.30
  83.2 1.9 collective-permute-start.2
  85.1 4.1 %collective-permute-start.3 = (f32[176,512]{1,0:T(8,128)S(1)}, f32[176,512]{1,0:T(8,128)S(1)}, u32[]{:S(2)}, u32[]{:S(2)}) collective-permute-start(f32[176,512]{1,0:T(8,128)S(1)} %get-tuple-element.9), channel_id=1, source_target_pairs={{1,0},{2,1},{3,2},{4,3},{5,4},{6,5},{7,6},{8,7},{9,8},{10,9},{11,1... | collective-permute-start | bytes 1081352 | tf_op jit(solution)/shard_map/ppermute | solution.py:26
  89.2 0.6 compare_select_fusion
  89.8 4.2 %collective-permute-done.2 = f32[176,512]{1,0:T(8,128)S(1)} collective-permute-done((f32[176,512]{1,0:T(8,128)S(1)}, f32[176,512]{1,0:T(8,128)S(1)}, u32[]{:S(2)}, u32[]{:S(2)}) %collective-permute-start.2) | collective-permute-done | bytes 360480 | tf_op jit(solution)/shard_map/ppermute | solution.py:25
  94.1 5.2 %collective-permute-done.3 = f32[176,512]{1,0:T(8,128)S(1)} collective-permute-done((f32[176,512]{1,0:T(8,128)S(1)}, f32[176,512]{1,0:T(8,128)S(1)}, u32[]{:S(2)}, u32[]{:S(2)}) %collective-permute-start.3) | collective-permute-done | bytes 360480 | tf_op jit(solution)/shard_map/ppermute | solution.py:26
  99.3 1.6 pad_maximum_fusion.1
  100.9 3.3 %copy.27 = f32[176,3072]{0,1:T(8,128)} copy(f32[176,3072]{1,0:T(8,128)} %pad_maximum_fusion.1) | data formatting | bytes 4325376 | tf_op jit(solution)/shard_map/concatenate | solution.py:27
  104.2 33.2 %gather_fusion.4 = f32[8192,176]{1,0:T(8,128)} fusion(f32[176,3072]{0,1:T(8,128)} %copy.27, s32[8192]{0:T(1024)S(1)} %broadcast_clamp_fusion.1), kind=kCustom, calls=%fused_computation.2.clone | custom fusion | bytes 11567104 | tf_op jit(solution)/shard_map/jit(_take)/gather | solution.py:55
  137.5 8.3 %copy.28 = f32[4,2048,176]{1,2,0:T(8,128)} copy(f32[4,2048,176]{2,1,0:T(8,128)} %bitcast.166) | data formatting | bytes 11534336 | tf_op jit(solution)/shard_map/jit(_take)/gather | solution.py:55
  145.7 6.9 %fusion.32 = f32[2048,176]{0,1:T(8,128)S(1)} fusion(f32[4,176,176]{2,1,0:T(8,128)S(1)} %copy-done, f32[4,2048,176]{1,2,0:T(8,128)} %copy.28, f32[4,2048]{1,0:T(4,128)S(1)} %bitcast_select_fusion, pred[4,2048]{1,0:T(4,128)(4,1)S(1)} %compare_and_fusion), kind=kOutput, calls=%fused_computation.46 | convolution fusion | flops 3047948288 | bytes 7745536 | tf_op jit(solution)/shard_map/fab,bfn->an/dot_general | solution.py:57
  152.6 1.9 fusion.22
  154.6 1.8 multiply_divide_fusion
  156.4 1.9 collective-permute-start.4
  158.3 3.9 %collective-permute-start.5 = (f32[56,512]{1,0:T(8,128)S(1)}, f32[56,512]{1,0:T(8,128)S(1)}, u32[]{:S(2)}, u32[]{:S(2)}) collective-permute-start(f32[56,512]{1,0:T(8,128)S(1)} %get-tuple-element.15), channel_id=1, source_target_pairs={{1,0},{2,1},{3,2},{4,3},{5,4},{6,5},{7,6},{8,7},{9,8},{10,9},{11,1... | collective-permute-start | bytes 344072 | tf_op jit(solution)/shard_map/ppermute | solution.py:26
  162.6 0.5 collective-permute-done.4
  163.1 5.2 %collective-permute-done.5 = f32[56,512]{1,0:T(8,128)S(1)} collective-permute-done((f32[56,512]{1,0:T(8,128)S(1)}, f32[56,512]{1,0:T(8,128)S(1)}, u32[]{:S(2)}, u32[]{:S(2)}) %collective-permute-start.5) | collective-permute-done | bytes 114720 | tf_op jit(solution)/shard_map/ppermute | solution.py:26
  168.4 0.5 copy.29
  168.9 27.8 %gather_fusion.5 = f32[8192,56]{1,0:T(8,128)} fusion(f32[56,3072]{0,1:T(8,128)S(1)} %copy.29, s32[8192]{0:T(1024)S(1)} %broadcast_clamp_fusion.1), kind=kCustom, calls=%fused_computation.1.clone | custom fusion | bytes 3702784 | tf_op jit(solution)/shard_map/jit(_take)/gather | solution.py:55
  196.6 3.7 %copy.30 = f32[4,2048,56]{1,2,0:T(8,128)} copy(f32[4,2048,56]{2,1,0:T(8,128)} %bitcast.168) | data formatting | bytes 3670016 | tf_op jit(solution)/shard_map/jit(_take)/gather | solution.py:55
  200.4 3.0 convolution_bitcast_fusion.3
  203.4 0.6 fusion.36
  204.0 0.4 multiply_divide_fusion.1
  204.4 1.9 collective-permute-start.6
  206.4 4.1 %collective-permute-start.7 = (f32[24,512]{1,0:T(8,128)S(1)}, f32[24,512]{1,0:T(8,128)S(1)}, u32[]{:S(2)}, u32[]{:S(2)}) collective-permute-start(f32[24,512]{1,0:T(8,128)S(1)} %get-tuple-element.17), channel_id=1, source_target_pairs={{1,0},{2,1},{3,2},{4,3},{5,4},{6,5},{7,6},{8,7},{9,8},{10,9},{11,1... | collective-permute-start | bytes 147464 | tf_op jit(solution)/shard_map/ppermute | solution.py:26
  210.6 5.1 %collective-permute-done.7 = f32[24,512]{1,0:T(8,128)S(1)} collective-permute-done((f32[24,512]{1,0:T(8,128)S(1)}, f32[24,512]{1,0:T(8,128)S(1)}, u32[]{:S(2)}, u32[]{:S(2)}) %collective-permute-start.7) | collective-permute-done | bytes 49184 | tf_op jit(solution)/shard_map/ppermute | solution.py:26
  215.7 0.5 copy.31
  216.2 27.8 %gather_fusion.2 = f32[8192,24]{1,0:T(8,128)} fusion(f32[24,3072]{0,1:T(8,128)S(1)} %copy.31, s32[8192]{0:T(1024)S(1)} %broadcast_clamp_fusion), kind=kCustom, calls=%fused_computation.6 | custom fusion | bytes 1605632 | tf_op jit(solution)/shard_map/jit(_take)/gather | solution.py:55
  243.9 8.3 %fusion.37 = f32[24,2048]{1,0:T(8,128)S(1)} fusion(f32[4,2048,24]{2,1,0:T(8,128)} %bitcast.169, f32[4,2048]{1,0:T(4,128)S(1)} %bitcast_select_fusion, pred[4,2048]{1,0:T(4,128)(4,1)S(1)} %compare_and_fusion, f32[4,24,24]{2,0,1:T(4,128)S(1)} %bitcast.180), kind=kOutput, calls=%fused_computation.56 | convolution fusion | flops 57016320 | bytes 1033216 | tf_op jit(solution)/shard_map/fab,bfn->an/dot_general | solution.py:57
  252.2 0.4 fusion.43
  252.7 0.8 fusion.46
  254.1 0.9 collective-permute-done.8
  255.2 1.3 collective-permute-start.9
  256.5 2.6 collective-permute-done.9
  259.2 1.1 fusion.40
  260.3 0.6 fusion.33
  260.9 1.9 collective-permute-start.10
  262.8 3.9 %collective-permute-start.11 = (f32[56,512]{1,0:T(8,128)S(1)}, f32[56,512]{1,0:T(8,128)S(1)}, u32[]{:S(2)}, u32[]{:S(2)}) collective-permute-start(f32[56,512]{1,0:T(8,128)S(1)} %get-tuple-element.13), channel_id=1, source_target_pairs={{1,0},{2,1},{3,2},{4,3},{5,4},{6,5},{7,6},{8,7},{9,8},{10,9},{11,1... | collective-permute-start | bytes 344072 | tf_op jit(solution)/shard_map/ppermute | solution.py:26
  266.7 1.3 fusion.28
  268.1 2.6 copy.34
  270.7 2.1 collective-permute-done.11
  272.8 0.9 pad_maximum_fusion.3
  273.7 1.6 copy.32
  275.3 27.8 %gather_fusion.6 = f32[8192,56]{1,0:T(8,128)} fusion(f32[56,3072]{0,1:T(8,128)S(1)} %copy.32, s32[8192]{0:T(1024)S(1)} %broadcast_clamp_fusion.1), kind=kCustom, calls=%fused_computation.3.clone | custom fusion | bytes 3702784 | tf_op jit(solution)/shard_map/jit(_take)/gather | solution.py:55
  303.0 2.9 copy.33
  305.9 1.5 convolution_bitcast_fusion.1
  307.4 1.4 fusion.26
  308.9 2.6 copy.35
  (72 shorter events, 3.1 us)
Async XLA Ops:
  0.6 10.4 %copy-start = (f32[4,176,176]{2,1,0:T(8,128)S(1)}, f32[4,176,176]{2,1,0:T(8,128)}, u32[]{:S(2)}) copy-start(f32[4,176,176]{2,1,0:T(8,128)} %param.24) | copy-start | bytes 1486852
  3.3 7.7 %copy-start.8 = (f32[56,176]{1,0:T(8,128)S(1)}, f32[56,176]{1,0:T(8,128)}, u32[]{:S(2)}) copy-start(f32[56,176]{1,0:T(8,128)} %param.26) | copy-start | bytes 118276
  3.3 9.9 %copy-start.11 = (s32[4,1,2048]{2,1,0:T(1,128)S(1)}, s32[4,1,2048]{2,1,0:T(1,128)}, u32[]{:S(2)}) copy-start(s32[4,1,2048]{2,1,0:T(1,128)} %param.20) | copy-start | bytes 98308
  4.2 9.0 %copy-start.17 = (f32[4,1,2048]{2,1,0:T(1,128)S(1)}, f32[4,1,2048]{2,1,0:T(1,128)}, u32[]{:S(2)}) copy-start(f32[4,1,2048]{2,1,0:T(1,128)} %param.19) | copy-start | bytes 98308
  4.2 9.1 %copy-start.9 = (f32[176,176]{1,0:T(8,128)S(1)}, f32[176,176]{1,0:T(8,128)}, u32[]{:S(2)}) copy-start(f32[176,176]{1,0:T(8,128)} %param.23) | copy-start | bytes 371716
  4.2 12.8 %collective-permute-start = (f32[176,512]{1,0:T(8,128)}, f32[176,512]{1,0:T(8,128)S(1)}, u32[]{:S(2)}, u32[]{:S(2)}) collective-permute-start(f32[176,512]{1,0:T(8,128)} %get-tuple-element.10), channel_id=1, source_target_pairs={{0,1},{1,2},{2,3},{3,4},{4,5},{5,6},{6,7},{7,8},{8,9},{9,10},{10,1... | collective-permute-start | bytes 1081352 | tf_op jit(solution)/shard_map/ppermute | solution.py:25
  9.1 15.4 %collective-permute-start.1 = (f32[176,512]{1,0:T(8,128)}, f32[176,512]{1,0:T(8,128)}, u32[]{:S(2)}, u32[]{:S(2)}) collective-permute-start(f32[176,512]{1,0:T(8,128)} %get-tuple-element.11), channel_id=1, source_target_pairs={{1,0},{2,1},{3,2},{4,3},{5,4},{6,5},{7,6},{8,7},{9,8},{10,9},{11,1... | collective-permute-start | bytes 1081352 | tf_op jit(solution)/shard_map/ppermute | solution.py:26
  11.6 3.4 %copy-start.14 = (f32[24,56]{1,0:T(8,128)S(1)}, f32[24,56]{1,0:T(8,128)}, u32[]{:S(2)}) copy-start(f32[24,56]{1,0:T(8,128)} %param.27) | copy-start | bytes 16132
  71.9 7.0 %copy-start.5 = (f32[176,1,2048]{2,1,0:T(1,128)S(1)}, f32[176,1,2048]{2,1,0:T(1,128)}, u32[]{:S(2)}) copy-start(f32[176,1,2048]{2,1,0:T(1,128)} %param.16) | copy-start | bytes 4325380
  71.9 7.0 %copy-start.6 = (f32[176,1,2048]{2,1,0:T(1,128)S(1)}, f32[176,1,2048]{2,1,0:T(1,128)}, u32[]{:S(2)}) copy-start(f32[176,1,2048]{2,1,0:T(1,128)} %param.17) | copy-start | bytes 4325380
  71.9 7.0 %copy-start.15 = (f32[1,2048]{1,0:T(1,128)S(1)}, f32[1,2048]{1,0:T(1,128)}, u32[]{:S(2)}) copy-start(f32[1,2048]{1,0:T(1,128)} %param.18) | copy-start | bytes 24580
  78.9 2.4 copy-start.18
  83.1 69.5 %copy-start.1 = (f32[176,2048]{1,0:T(8,128)}, f32[176,2048]{1,0:T(8,128)S(1)}, u32[]{:S(2)}) copy-start(f32[176,2048]{1,0:T(8,128)S(1)} %fusion.30) | copy-start | bytes 4325380
  83.2 10.9 %collective-permute-start.2 = (f32[176,512]{1,0:T(8,128)S(1)}, f32[176,512]{1,0:T(8,128)S(1)}, u32[]{:S(2)}, u32[]{:S(2)}) collective-permute-start(f32[176,512]{1,0:T(8,128)S(1)} %get-tuple-element.8), channel_id=1, source_target_pairs={{0,1},{1,2},{2,3},{3,4},{4,5},{5,6},{6,7},{7,8},{8,9},{9,10},{10,1... | collective-permute-start | bytes 1081352 | tf_op jit(solution)/shard_map/ppermute | solution.py:25
  85.1 14.2 %collective-permute-start.3 = (f32[176,512]{1,0:T(8,128)S(1)}, f32[176,512]{1,0:T(8,128)S(1)}, u32[]{:S(2)}, u32[]{:S(2)}) collective-permute-start(f32[176,512]{1,0:T(8,128)S(1)} %get-tuple-element.9), channel_id=1, source_target_pairs={{1,0},{2,1},{3,2},{4,3},{5,4},{6,5},{7,6},{8,7},{9,8},{10,9},{11,1... | collective-permute-start | bytes 1081352 | tf_op jit(solution)/shard_map/ppermute | solution.py:26
  145.7 6.9 %copy-start.7 = (f32[176,1,2048]{2,1,0:T(1,128)S(1)}, f32[176,1,2048]{2,1,0:T(1,128)}, u32[]{:S(2)}) copy-start(f32[176,1,2048]{2,1,0:T(1,128)} %param.17) | copy-start | bytes 4325380
  154.6 1.8 copy-start.3
  156.4 6.7 %collective-permute-start.4 = (f32[56,512]{1,0:T(8,128)S(1)}, f32[56,512]{1,0:T(8,128)S(1)}, u32[]{:S(2)}, u32[]{:S(2)}) collective-permute-start(f32[56,512]{1,0:T(8,128)S(1)} %get-tuple-element.14), channel_id=1, source_target_pairs={{0,1},{1,2},{2,3},{3,4},{4,5},{5,6},{6,7},{7,8},{8,9},{9,10},{10,1... | collective-permute-start | bytes 344072 | tf_op jit(solution)/shard_map/ppermute | solution.py:25
  158.3 10.0 %collective-permute-start.5 = (f32[56,512]{1,0:T(8,128)S(1)}, f32[56,512]{1,0:T(8,128)S(1)}, u32[]{:S(2)}, u32[]{:S(2)}) collective-permute-start(f32[56,512]{1,0:T(8,128)S(1)} %get-tuple-element.15), channel_id=1, source_target_pairs={{1,0},{2,1},{3,2},{4,3},{5,4},{6,5},{7,6},{8,7},{9,8},{10,9},{11,1... | collective-permute-start | bytes 344072 | tf_op jit(solution)/shard_map/ppermute | solution.py:26
  200.4 3.0 copy-start.12
  203.4 7.1 %copy-start.16 = (s32[4,2048,1]{1,2,0:T(1,128)S(1)}, s32[4,2048,1]{1,2,0:T(1,128)}, u32[]{:S(2)}) copy-start(s32[4,2048,1]{1,2,0:T(1,128)} %compare_select_fusion) | copy-start | bytes 98308
  204.4 6.1 %collective-permute-start.6 = (f32[24,512]{1,0:T(8,128)S(1)}, f32[24,512]{1,0:T(8,128)S(1)}, u32[]{:S(2)}, u32[]{:S(2)}) collective-permute-start(f32[24,512]{1,0:T(8,128)S(1)} %get-tuple-element.16), channel_id=1, source_target_pairs={{0,1},{1,2},{2,3},{3,4},{4,5},{5,6},{6,7},{7,8},{8,9},{9,10},{10,1... | collective-permute-start | bytes 147464 | tf_op jit(solution)/shard_map/ppermute | solution.py:25
  206.4 9.3 %collective-permute-start.7 = (f32[24,512]{1,0:T(8,128)S(1)}, f32[24,512]{1,0:T(8,128)S(1)}, u32[]{:S(2)}, u32[]{:S(2)}) collective-permute-start(f32[24,512]{1,0:T(8,128)S(1)} %get-tuple-element.17), channel_id=1, source_target_pairs={{1,0},{2,1},{3,2},{4,3},{5,4},{6,5},{7,6},{8,7},{9,8},{10,9},{11,1... | collective-permute-start | bytes 147464 | tf_op jit(solution)/shard_map/ppermute | solution.py:26
  243.9 8.7 %copy-start.19 = (s32[1,2048]{1,0:T(1,128)S(1)}, s32[1,2048]{1,0:T(1,128)}, u32[]{:S(2)}) copy-start(s32[1,2048]{1,0:T(1,128)} %param.21) | copy-start | bytes 24580
  252.6 7.6 %copy-start.13 = (f32[56,2048]{1,0:T(8,128)S(1)}, f32[56,2048]{1,0:T(8,128)}, u32[]{:S(2)}) copy-start(f32[56,2048]{1,0:T(8,128)} %get-tuple-element.22) | copy-start | bytes 1376260
  253.7 1.3 collective-permute-start.8
  255.2 3.9 %collective-permute-start.9 = (f32[24,256]{1,0:T(8,128)S(1)}, f32[24,256]{1,0:T(8,128)S(1)}, u32[]{:S(2)}, u32[]{:S(2)}) collective-permute-start(f32[24,256]{1,0:T(8,128)S(1)} %fusion.50), channel_id=1, source_target_pairs={{0,64},{64,0},{32,96},{96,32},{128,192},{192,128},{160,224},{224,1... | collective-permute-start | bytes 73736 | tf_op jit(solution)/shard_map/ppermute | solution.py:38
  260.2 6.5 %copy-start.2 = (f32[176,2048]{1,0:T(8,128)S(1)}, f32[176,2048]{1,0:T(8,128)}, u32[]{:S(2)}) copy-start(f32[176,2048]{1,0:T(8,128)} %copy-done.1) | copy-start | bytes 4325380
  260.9 9.8 %collective-permute-start.10 = (f32[56,512]{1,0:T(8,128)S(1)}, f32[56,512]{1,0:T(8,128)S(1)}, u32[]{:S(2)}, u32[]{:S(2)}) collective-permute-start(f32[56,512]{1,0:T(8,128)S(1)} %get-tuple-element.12), channel_id=1, source_target_pairs={{0,1},{1,2},{2,3},{3,4},{4,5},{5,6},{6,7},{7,8},{8,9},{9,10},{10,1... | collective-permute-start | bytes 344072 | tf_op jit(solution)/shard_map/ppermute | solution.py:25
  262.8 10.0 %collective-permute-start.11 = (f32[56,512]{1,0:T(8,128)S(1)}, f32[56,512]{1,0:T(8,128)S(1)}, u32[]{:S(2)}, u32[]{:S(2)}) collective-permute-start(f32[56,512]{1,0:T(8,128)S(1)} %get-tuple-element.13), channel_id=1, source_target_pairs={{1,0},{2,1},{3,2},{4,3},{5,4},{6,5},{7,6},{8,7},{9,8},{10,9},{11,1... | collective-permute-start | bytes 344072 | tf_op jit(solution)/shard_map/ppermute | solution.py:26
  303.0 2.9 copy-start.10
  305.9 1.5 copy-start.4
where the time goes:
time: 312 us; the launch traced here: 311 us
  local copies, waits for them, and re-layouts  190 us (61%)
  matrix products  45.9 us (15%)
  waiting for transfers between devices  33.7 us (11%)
  starting transfers between devices  31.9 us (10%)
  other arithmetic  7.84 us (3%)
    gather x9, local copies, waits for them, and re-layouts, face_sum(): picked = jnp.take(extended, target, axis=1)  173 us
    dot_general x5, matrix products, face_sum(): jnp.einsum('fab,bfn->an', fluxes, picked * weights[None], precision=PRECISE)  26.6 us
    ppermute x5, waiting for transfers between devices, padded(): after = lax.ppermute(first, axis, down)  25.2 us
    dot_general x24, matrix products, product(): jnp.dot(former, latter, precision=PRECISE, preferred_element_type=jnp.flo...  19.3 us
    ppermute x5, starting transfers between devices, padded(): after = lax.ppermute(first, axis, down)  18 us
    ppermute x5, starting transfers between devices, padded(): before = lax.ppermute(last, axis, up)  12.5 us
    concatenate x5, local copies, waits for them, and re-layouts, padded(): value = jnp.concatenate([before, value, after], axis=dim)  9.16 us
  transfers between devices with their start and end apart: 12, of which 10 were waited for; matrix products, arithmetic and copies ran while one was open for 3% of the time, Pallas kernels for 0%

commit v1 on v0

v1 whole, which is shorter than its diff:
```python
from functools import partial

import jax
import jax.numpy as jnp
from jax import lax
from jax.experimental import pallas as pl
from jax.experimental.pallas import tpu as pltpu
from jax.sharding import PartitionSpec as P

NP0, NP1, NP2 = 176, 56, 24
FACES = 4
AGG = 8
HLEV = 2
HALO = 512
EC_DEV = 256
E_DEV = 2048
LANES = 128
PAIR = 256
PAIRS = E_DEV // PAIR
SIDE = HALO // PAIR
SPAN = 2 * SIDE + 1
EXT = PAIRS + 2 * SIDE
ROWS_PER = E_DEV // LANES
DAMPING = 0.8
KF = 896
KM = 288
KL = 128
NPM = 64
NPL = 32
MESH = pl.DeviceIdType.MESH
F32, BF16 = jnp.float32, jnp.bfloat16
NN = (((1,), (0,)), ((), ()))
NT = (((1,), (1,)), ((), ()))


def exact(a, b, dims=NN):
    return lax.dot_general(a, b, dims, precision=lax.Precision.HIGHEST, preferred_element_type=F32)


def parts(x):
    high = x.astype(BF16)
    low = (x - high.astype(F32)).astype(BF16)
    return high, low


def store_parts(ref, x, rows):
    high, low = parts(x)
    ref[pl.ds(0, x.shape[0]), :] = high
    ref[pl.ds(rows, x.shape[0]), :] = low


def product(split_ref, rows, high, low):
    both = jnp.dot(split_ref[...], high, preferred_element_type=F32)
    rest = jnp.dot(split_ref[pl.ds(0, rows), :], low, preferred_element_type=F32)
    return both[:rows] + both[rows:] + rest


def kernel(
    n_dom,
    n_fold,
    iter_ref,
    rhs_ref,
    jac_ref,
    scale_ref,
    offset_ref,
    agg_ref,
    live_ref,
    stiff_ref,
    flux_ref,
    smoother_ref,
    rmid_ref,
    rlow_ref,
    upd_ref,
    res_ref,
    e1,
    e2,
    e3,
    e4,
    e5,
    split1,
    split2,
    pick,
    second,
    mid_rhs,
    low_rhs,
    low_res,
    feed_high,
    feed_low,
    fine_f32,
    fine_split,
    smooth_split,
    rmid_split,
    mid_f32,
    mid_split,
    lift_f32,
    lift_split,
    low_f32,
    low_split,
    rmid_t_split,
    swap_out,
    swap_in,
    send_sem,
    recv_sem,
    swap_send,
    swap_recv,
):
    me = lax.axis_index("dom")
    fold = lax.axis_index("fold")
    right = lax.rem(me + 1, n_dom)
    left = lax.rem(me + n_dom - 1, n_dom)
    partners = []
    for height in range(HLEV):
        step = 2**height
        bit = (fold // step) % 2
        partners.append(fold + step - 2 * step * bit)

    barrier = pltpu.get_barrier_semaphore()
    for other in (left, right):
        pl.semaphore_signal(barrier, inc=1, device_id={"dom": other}, device_id_type=MESH)
    for other in partners:
        pl.semaphore_signal(barrier, inc=1, device_id={"fold": other}, device_id_type=MESH)

    lane = lax.broadcasted_iota(jnp.int32, (1, PAIR), 1)
    live = live_ref[0, 0]

    def row_of(ref, base, u):
        return jnp.concatenate(
            [ref[pl.ds(base + 2 * u, 1), :], ref[pl.ds(base + 2 * u + 1, 1), :]], axis=1
        )

    def active_of(u):
        return jnp.where(u * PAIR + lane < live, 1.0, 0.0).astype(F32)

    def jac_of(u):
        return row_of(jac_ref, 0, u)

    def weight_of(f, u):
        offset = row_of(offset_ref, f * ROWS_PER, u)
        target = me * E_DEV + u * PAIR + lane + offset
        inside = (offset != 0) & (target >= 0) & (target < n_dom * E_DEV)
        return jnp.where(inside, row_of(scale_ref, f * ROWS_PER, u), 0.0)

    def wide(ref, u):
        return jnp.concatenate(
            [ref[pl.ds(2 * u + h, NP0, stride=ROWS_PER), :] for h in range(2)], axis=1
        )

    def put_wide(ref, u, value):
        for h in range(2):
            ref[pl.ds(2 * u + h, NP0, stride=ROWS_PER), :] = value[:, h * LANES : (h + 1) * LANES]

    def exchange(k, buffer):
        to_right = pltpu.make_async_remote_copy(
            src_ref=buffer.at[pl.ds(PAIRS, SIDE)],
            dst_ref=buffer.at[pl.ds(0, SIDE)],
            send_sem=send_sem.at[k, 0],
            recv_sem=recv_sem.at[k, 0],
            device_id={"dom": right},
            device_id_type=MESH,
        )
        to_left = pltpu.make_async_remote_copy(
            src_ref=buffer.at[pl.ds(SIDE, SIDE)],
            dst_ref=buffer.at[pl.ds(SIDE + PAIRS, SIDE)],
            send_sem=send_sem.at[k, 1],
            recv_sem=recv_sem.at[k, 1],
            device_id={"dom": left},
            device_id_type=MESH,
        )
        to_right.start()
        to_left.start()
        return to_right, to_left

    def finish(copies):
        for copy in copies:
            copy.wait()

    def over(first, last, body):
        lax.fori_loop(first, last, lambda i, c: (body(i), c)[1], 0)

    def over_edges(body):
        lax.fori_loop(
            0, 2 * SIDE, lambda i, c: (body(i + (i // SIDE) * (PAIRS - 2 * SIDE)), c)[1], 0
        )

    def mask_block(u):
        e1[u + SIDE] = active_of(u) * wide(iter_ref, u)

    over(0, PAIRS, mask_block)
    pl.semaphore_wait(barrier, 2 + HLEV)
    first_halo = exchange(0, e1)

    def split_block(source, target, b):
        store_parts(target.at[b], source[b], NP0)

    def split_halo(source, target):
        for b in (*range(SIDE), *range(SIDE + PAIRS, EXT)):
            split_block(source, target, b)

    over(SIDE, SIDE + PAIRS, lambda b: split_block(e1, split1, b))

    fine_f32[...] = jnp.zeros_like(fine_f32)
    for f in range(FACES):
        fine_f32[:, f * NP0 : (f + 1) * NP0] = flux_ref[f]
    fine_f32[:, FACES * NP0 : (FACES + 1) * NP0] = stiff_ref[...]
    store_parts(fine_split, fine_f32[...], NP0)
    store_parts(smooth_split, smoother_ref[...], NP0)
    feed_high[...] = jnp.zeros_like(feed_high)
    feed_low[...] = jnp.zeros_like(feed_low)

    def build_pick(u, f):
        reach = lane + row_of(offset_ref, f * ROWS_PER, u) + HALO
        rows = lax.broadcasted_iota(jnp.int32, (PAIR, PAIR), 0)
        for j in range(SPAN):
            pick[u, f, pl.ds(j * PAIR, PAIR), :] = jnp.where(
                rows + j * PAIR == reach, 1.0, 0.0
            ).astype(BF16)

    def fine_apply(u, source, split, build):
        around = jnp.concatenate([split[u + j] for j in range(SPAN)], axis=1)
        for f in range(FACES):
            if build:
                build_pick(u, f)
            both = jnp.dot(around, pick[u, f], preferred_element_type=F32)
            high, low = parts((both[:NP0] + both[NP0:]) * weight_of(f, u))
            feed_high[pl.ds(f * NP0, NP0), :] = high
            feed_low[pl.ds(f * NP0, NP0), :] = low
        high, low = parts(jac_of(u) * source[u + SIDE])
        feed_high[pl.ds(FACES * NP0, NP0), :] = high
        feed_low[pl.ds(FACES * NP0, NP0), :] = low
        return product(fine_split, NP0, feed_high[...], feed_low[...])

    def smooth_block(u):
        active = active_of(u)
        first_res = active * (wide(rhs_ref, u) - fine_apply(u, e1, split1, True))
        high, low = parts(first_res)
        update = product(smooth_split, NP0, high, low)
        block = e1[u + SIDE] + update * (active / jac_of(u))
        e2[u + SIDE] = block
        store_parts(split2.at[u + SIDE], block, NP0)

    over(SIDE, PAIRS - SIDE, smooth_block)
    finish(first_halo)
    split_halo(e1, split1)
    over_edges(smooth_block)
    second_halo = exchange(1, e2)

    rmid = rmid_ref[...]
    rlow = rlow_ref[...]
    mid_f32[...] = jnp.zeros_like(mid_f32)
    lift_f32[...] = jnp.zeros_like(lift_f32)
    low_f32[...] = jnp.zeros_like(low_f32)
    rmid_split[...] = jnp.zeros_like(rmid_split)
    store_parts(rmid_split, rmid, NPM)

    def identity(n):
        rows = lax.broadcasted_iota(jnp.int32, (n, n), 0)
        cols = lax.broadcasted_iota(jnp.int32, (n, n), 1)
        return jnp.where(rows == cols, 1.0, 0.0).astype(F32)

    for f in range(FACES + 1):
        matrix = flux_ref[f] if f < FACES else stiff_ref[...]
        mid_matrix = exact(exact(rmid, matrix), rmid, NT)
        mid_f32[0:NP1, f * NP1 : (f + 1) * NP1] = mid_matrix
        lift_f32[:, f * NP1 : (f + 1) * NP1] = exact(matrix, rmid, NT)
        low_matrix = exact(exact(rlow, mid_matrix), rlow, NT)
        low_f32[0:NP2, f * NP2 : (f + 1) * NP2] = low_matrix
    stiff_low = low_matrix
    diag_mid = jnp.sum(mid_matrix * identity(NP1), axis=1, keepdims=True)
    diag_low = jnp.sum(low_matrix * identity(NP2), axis=1, keepdims=True)
    store_parts(mid_split, mid_f32[...], NPM)
    store_parts(lift_split, lift_f32[...], NP0)
    store_parts(low_split, low_f32[...], NPL)
    rmid_t_split[...] = jnp.zeros_like(rmid_t_split)
    rmid_t_high, rmid_t_low = parts(exact(identity(NP0), rmid, NT))
    rmid_t_split[pl.ds(0, NP0), 0:NP1] = rmid_t_high
    rmid_t_split[pl.ds(NP0, NP0), 0:NP1] = rmid_t_low
    rlow_t = exact(identity(NP1), rlow, NT)

    def second_block(u):
        active = active_of(u)
        block = active * (wide(rhs_ref, u) - fine_apply(u, e2, split2, False))
        second[u] = block
        high, low = parts(block)
        rhs = product(rmid_split, NPM, high, low)[:NP1]
        mid_rhs[u] = rhs
        e3[u + SIDE] = rhs * (DAMPING * active / jac_of(u)) / diag_mid

    over(SIDE, PAIRS - SIDE, second_block)
    finish(second_halo)
    split_halo(e2, split2)
    over_edges(second_block)
    mid_halo = exchange(2, e3)

    def gathered(u, buffer, rows, padding):
        reach_lane = lax.broadcasted_iota(jnp.int32, (8, LANES), 1)
        pieces = []
        for f in range(FACES):
            halves = []
            for h in range(2):
                offset = offset_ref[pl.ds(f * ROWS_PER + 2 * u + h, 1), :]
                reach = jnp.broadcast_to(offset, (8, LANES)) + reach_lane + HALO
                inner = reach & (LANES - 1)
                outer = reach >> 7
                groups = []
                for g in range(rows // 8):
                    value = jnp.zeros((8, LANES), F32)
                    for j in range(2 * HALO // LANES + 1):
                        b = h + j
                        source = buffer[
                            u + b // 2, pl.ds(8 * g, 8), pl.ds((b % 2) * LANES, LANES)
                        ]
                        found = jnp.take_along_axis(source, inner, axis=1)
                        value = jnp.where(outer == j, found, value)
                    groups.append(value)
                halves.append(jnp.concatenate(groups, axis=0))
            pieces.append(jnp.concatenate(halves, axis=1) * weight_of(f, u))
        pieces.append(jac_of(u) * buffer[u + SIDE])
        pieces.append(jnp.zeros((padding, PAIR), F32))
        return parts(jnp.concatenate(pieces, axis=0))

    def mid_block(u):
        active = active_of(u)
        high, low = gathered(u, e3, NP1, KM - 5 * NP1)
        mid_res = mid_rhs[u] - active * product(mid_split, NPM, high, low)[:NP1]
        rhs = exact(rlow, mid_res)
        low_rhs[u] = rhs
        e4[u + SIDE] = rhs * (DAMPING * active / jac_of(u)) / diag_low

    over(SIDE, PAIRS - SIDE, mid_block)
    finish(mid_halo)
    over_edges(mid_block)
    low_halo = exchange(3, e4)

    def low_block(u):
        active = active_of(u)
        high, low = gathered(u, e4, NP2, KL - 5 * NP2)
        low_res[u] = low_rhs[u] - active * product(low_split, NPL, high, low)[:NP2]

    over(SIDE, PAIRS - SIDE, low_block)
    finish(low_halo)
    over_edges(low_block)

    def members(u):
        rows = lax.broadcasted_iota(jnp.int32, (EC_DEV, PAIR), 0)
        return jnp.where(rows == row_of(agg_ref, 0, u), 1.0, 0.0).astype(BF16)

    def coarse_block(u, total):
        high, low = parts(
            jnp.concatenate([low_res[u], jnp.zeros((NPL - NP2, PAIR), F32)], axis=0)
        )
        both = lax.dot_general(
            jnp.concatenate([high, low], axis=0), members(u), NT, preferred_element_type=F32
        )
        return total + both[:NP2] + both[NPL : NPL + NP2]

    coarse = lax.fori_loop(0, PAIRS, coarse_block, jnp.zeros((NP2, EC_DEV), F32))
    sections = []
    for height in range(HLEV):
        scaled = coarse / diag_low
        sections.append(scaled * (DAMPING / (AGG * 2**height)))
        residue = coarse - DAMPING * exact(stiff_low, scaled)
        swap_out[height] = residue
        copy = pltpu.make_async_remote_copy(
            src_ref=swap_out.at[height],
            dst_ref=swap_in.at[height],
            send_sem=swap_send.at[height],
            recv_sem=swap_recv.at[height],
            device_id={"fold": partners[height]},
            device_id_type=MESH,
        )
        copy.start()
        copy.wait()
        coarse = residue + swap_in[height]
    corr = coarse / diag_low * (DAMPING / (AGG * 2**HLEV))
    for height in reversed(range(HLEV)):
        corr = sections[height] + corr
    corr_high, corr_low = parts(jnp.concatenate([corr, jnp.zeros((NPL - NP2, EC_DEV), F32)], axis=0))
    corr_split = jnp.concatenate([corr_high, corr_low], axis=0)

    def ascend_block(u):
        active = active_of(u)
        both = jnp.dot(corr_split, members(u), preferred_element_type=F32)
        low_total = e4[u + SIDE] + active * (both[:NP2] + both[NPL : NPL + NP2])
        e5[u + SIDE] = e3[u + SIDE] + exact(rlow_t, low_total)

    over(0, PAIRS, ascend_block)
    last_halo = exchange(4, e5)

    def update_block(u):
        high, low = parts(
            jnp.concatenate([e5[u + SIDE], jnp.zeros((NPM - NP1, PAIR), F32)], axis=0)
        )
        put_wide(upd_ref, u, e2[u + SIDE] + product(rmid_t_split, NP0, high, low))

    over(0, PAIRS, update_block)

    def residual_block(u):
        high, low = gathered(u, e5, NP1, KM - 5 * NP1)
        put_wide(res_ref, u, second[u] - active_of(u) * product(lift_split, NP0, high, low))

    over(SIDE, PAIRS - SIDE, residual_block)
    finish(last_halo)
    over_edges(residual_block)


def on_device(
    n_dom,
    n_fold,
    iterate,
    right_side,
    jacobian,
    face_scale,
    face_offset,
    agglomerate,
    live_count,
    stiff_fine,
    flux_fine,
    smoother,
    restrict_mid,
    restrict_low,
):
    def flat(array):
        return array.reshape(-1, LANES)

    vmem = pl.BlockSpec(memory_space=pltpu.VMEM)
    smem = pl.BlockSpec(memory_space=pltpu.SMEM)
    out = jax.ShapeDtypeStruct((NP0 * ROWS_PER, LANES), F32)
    updated, residual = pl.pallas_call(
        partial(kernel, n_dom, n_fold),
        out_shape=(out, out),
        in_specs=[vmem] * 6 + [smem] + [vmem] * 5,
        out_specs=(vmem, vmem),
        scratch_shapes=[
            pltpu.VMEM((EXT, NP0, PAIR), F32),
            pltpu.VMEM((EXT, NP0, PAIR), F32),
            pltpu.VMEM((EXT, NP1, PAIR), F32),
            pltpu.VMEM((EXT, NP2, PAIR), F32),
            pltpu.VMEM((EXT, NP1, PAIR), F32),
            pltpu.VMEM((EXT, 2 * NP0, PAIR), BF16),
            pltpu.VMEM((EXT, 2 * NP0, PAIR), BF16),
            pltpu.VMEM((PAIRS, FACES, SPAN * PAIR, PAIR), BF16),
            pltpu.VMEM((PAIRS, NP0, PAIR), F32),
            pltpu.VMEM((PAIRS, NP1, PAIR), F32),
            pltpu.VMEM((PAIRS, NP2, PAIR), F32),
            pltpu.VMEM((PAIRS, NP2, PAIR), F32),
            pltpu.VMEM((KF, PAIR), BF16),
            pltpu.VMEM((KF, PAIR), BF16),
            pltpu.VMEM((NP0, KF), F32),
            pltpu.VMEM((2 * NP0, KF), BF16),
            pltpu.VMEM((2 * NP0, NP0), BF16),
            pltpu.VMEM((2 * NPM, NP0), BF16),
            pltpu.VMEM((NPM, KM), F32),
            pltpu.VMEM((2 * NPM, KM), BF16),
            pltpu.VMEM((NP0, KM), F32),
            pltpu.VMEM((2 * NP0, KM), BF16),
            pltpu.VMEM((NPL, KL), F32),
            pltpu.VMEM((2 * NPL, KL), BF16),
            pltpu.VMEM((2 * NP0, NPM), BF16),
            pltpu.VMEM((HLEV, NP2, EC_DEV), F32),
            pltpu.VMEM((HLEV, NP2, EC_DEV), F32),
            pltpu.SemaphoreType.DMA((5, 2)),
            pltpu.SemaphoreType.DMA((5, 2)),
            pltpu.SemaphoreType.DMA((HLEV,)),
            pltpu.SemaphoreType.DMA((HLEV,)),
        ],
        compiler_params=pltpu.CompilerParams(
            collective_id=0, has_side_effects=True, vmem_limit_bytes=60 * 1024 * 1024
        ),
    )(
        flat(iterate),
        flat(right_side),
        flat(jacobian),
        flat(face_scale),
        flat(face_offset),
        flat(agglomerate),
        live_count,
        stiff_fine,
        flux_fine,
        smoother,
        restrict_mid,
        restrict_low,
    )
    return updated.reshape(iterate.shape), residual.reshape(iterate.shape)


def solution(mesh):
    return jax.shard_map(
        partial(on_device, mesh.shape["dom"], mesh.shape["fold"]),
        mesh=mesh,
        in_specs=(
            P(None, "fold", "dom"),
            P(None, "fold", "dom"),
            P("fold", "dom"),
            P(None, "fold", "dom"),
            P(None, "fold", "dom"),
            P("fold", "dom"),
            P("fold", "dom"),
            P(),
            P(),
            P(),
            P(),
            P(),
        ),
        out_specs=(P(None, "fold", "dom"), P(None, "fold", "dom")),
        check_vma=False,
    )
```

time: 312 us -> 91.9 us (0.29)
  the two profiles are of different devices: /device:TPU:124 before, /device:TPU:1 now
where the time goes in v1:
time: 91.9 us; the launch traced here: 91.7 us
  Pallas kernels  85.8 us (93%)
  local copies, waits for them, and re-layouts  4.66 us (5%)
  between operations  1.3 us (1%)
    pallas_call x1, Pallas kernels, on_device(): pl.pallas_call(partial(kernel, n_dom, n_fold), out_shape=(out, out), in_s...  85.8 us
    unnamed x4, local copies, waits for them, and re-layouts  4.66 us

profile of v1, /device:TPU:1, one launch (start us, length us, event | category | flops | bytes accessed | tf_op | source)
XLA Modules:
  0.0 91.7 jit_solution(5582940575921881530)
XLA Ops:
  1.3 85.8 %shard_map.131 = (f32[2816,128]{1,0:T(8,128)}, f32[2816,128]{1,0:T(8,128)}) custom-call(f32[2816,128]{1,0:T(8,128)} %bitcast.8, f32[2816,128]{1,0:T(8,128)} %bitcast.9, f32[16,128]{1,0:T(8,128)} %bitcast.14, f32[64,128]{1,0:T(8,128)} %bitcast.12, s32[64,128]{1,0:T(8,128)} %bitcast.13, s32[16,128]{1,0:T(8,128)} %bitcast.15, s32[1,1]{1,0:T(1,128)S(6)} %copy.18.live_ref, ...), custom_call_target="tpu_custom_call" | custom-call | tf_op jit(solution)/shard_map/pallas_call | solution.py:428
  87.1 0.0 copy-start
  87.1 3.6 %copy.19 = f32[176,1,2048]{2,1,0:T(1,128)} copy(f32[176,1,2048]{2,1,0:T(1,128)} %bitcast.11) | data formatting | bytes 2883584
  90.6 0.0 copy-done
  90.6 1.1 %copy.20 = f32[176,1,2048]{2,1,0:T(1,128)} copy(f32[176,1,2048]{2,1,0:T(1,128)S(1)} %bitcast.10) | data formatting | bytes 2883584
Async XLA Ops:
  87.1 3.6 %copy-start = (f32[2816,128]{1,0:T(8,128)S(1)}, f32[2816,128]{1,0:T(8,128)}, u32[]{:S(2)}) copy-start(f32[2816,128]{1,0:T(8,128)} %get-tuple-element.5) | copy-start | bytes 4325380

commit v2 on v1

--- a/solution.py
+++ b/solution.py
@@ -22,11 +22,13 @@
 EXT = PAIRS + 2 * SIDE
 ROWS_PER = E_DEV // LANES
 DAMPING = 0.8
-KF = 896
-KM = 288
-KL = 128
 NPM = 64
 NPL = 32
+KF = 896
+KM = 5 * NPM
+KL = 5 * NPL
+MX_ROWS = 112
+MX_FACES = 2
 MESH = pl.DeviceIdType.MESH
 F32, BF16 = jnp.float32, jnp.bfloat16
 NN = (((1,), (0,)), ((), ()))
@@ -81,22 +83,26 @@
     split2,
     pick,
     second,
+    split3,
+    split5,
     mid_rhs,
     low_rhs,
     low_res,
     feed_high,
     feed_low,
+    feed_mid,
+    feed_coarse,
     fine_f32,
     fine_split,
     smooth_split,
     rmid_split,
-    mid_f32,
+    rboth_split,
     mid_split,
     lift_f32,
     lift_split,
-    low_f32,
     low_split,
     rmid_t_split,
+    low_t_f32,
     swap_out,
     swap_in,
     send_sem,
@@ -190,10 +196,16 @@
     first_halo = exchange(0, e1)
 
     def split_block(source, target, b):
-        store_parts(target.at[b], source[b], NP0)
+        store_parts(target.at[b], source[b, pl.ds(0, MX_ROWS), :], MX_ROWS)
+
+    def split_mid(target, b, value):
+        padded = jnp.concatenate([value, jnp.zeros((NPM - NP1, PAIR), F32)], axis=0)
+        store_parts(target.at[b], padded, NPM)
+
+    halo_blocks = (*range(SIDE), *range(SIDE + PAIRS, EXT))
 
     def split_halo(source, target):
-        for b in (*range(SIDE), *range(SIDE + PAIRS, EXT)):
+        for b in halo_blocks:
             split_block(source, target, b)
 
     over(SIDE, SIDE + PAIRS, lambda b: split_block(e1, split1, b))
@@ -215,15 +227,45 @@
                 rows + j * PAIR == reach, 1.0, 0.0
             ).astype(BF16)
 
+    reach_lane = lax.broadcasted_iota(jnp.int32, (8, LANES), 1)
+
+    def lane_gather(u, buffer, f, first, rows, padding=0):
+        halves = []
+        for h in range(2):
+            offset = offset_ref[pl.ds(f * ROWS_PER + 2 * u + h, 1), :]
+            reach = jnp.broadcast_to(offset, (8, LANES)) + reach_lane + HALO
+            inner = reach & (LANES - 1)
+            outer = reach >> 7
+            groups = []
+            for g in range(rows // 8):
+                value = None
+                for j in range(2 * HALO // LANES + 1):
+                    b = h + j
+                    source = buffer[
+                        u + b // 2, pl.ds(first + 8 * g, 8), pl.ds((b % 2) * LANES, LANES)
+                    ]
+                    found = jnp.take_along_axis(source, inner, axis=1)
+                    value = found if j == 0 else jnp.where(outer == j, found, value)
+                groups.append(value)
+            if padding:
+                groups.append(jnp.zeros((padding, LANES), F32))
+            halves.append(jnp.concatenate(groups, axis=0))
+        return jnp.concatenate(halves, axis=1)
+
     def fine_apply(u, source, split, build):
         around = jnp.concatenate([split[u + j] for j in range(SPAN)], axis=1)
         for f in range(FACES):
             if build:
                 build_pick(u, f)
+            weight = weight_of(f, u)
             both = jnp.dot(around, pick[u, f], preferred_element_type=F32)
-            high, low = parts((both[:NP0] + both[NP0:]) * weight_of(f, u))
-            feed_high[pl.ds(f * NP0, NP0), :] = high
-            feed_low[pl.ds(f * NP0, NP0), :] = low
+            high, low = parts((both[:MX_ROWS] + both[MX_ROWS:]) * weight)
+            feed_high[pl.ds(f * NP0, MX_ROWS), :] = high
+            feed_low[pl.ds(f * NP0, MX_ROWS), :] = low
+            rest = lane_gather(u, source, f, MX_ROWS, NP0 - MX_ROWS)
+            high, low = parts(rest * weight)
+            feed_high[pl.ds(f * NP0 + MX_ROWS, NP0 - MX_ROWS), :] = high
+            feed_low[pl.ds(f * NP0 + MX_ROWS, NP0 - MX_ROWS), :] = low
         high, low = parts(jac_of(u) * source[u + SIDE])
         feed_high[pl.ds(FACES * NP0, NP0), :] = high
         feed_low[pl.ds(FACES * NP0, NP0), :] = low
@@ -236,7 +278,7 @@
         update = product(smooth_split, NP0, high, low)
         block = e1[u + SIDE] + update * (active / jac_of(u))
         e2[u + SIDE] = block
-        store_parts(split2.at[u + SIDE], block, NP0)
+        store_parts(split2.at[u + SIDE], block[:MX_ROWS], MX_ROWS)
 
     over(SIDE, PAIRS - SIDE, smooth_block)
     finish(first_halo)
@@ -246,35 +288,53 @@
 
     rmid = rmid_ref[...]
     rlow = rlow_ref[...]
-    mid_f32[...] = jnp.zeros_like(mid_f32)
+    rboth = exact(rlow, rmid)
     lift_f32[...] = jnp.zeros_like(lift_f32)
-    low_f32[...] = jnp.zeros_like(low_f32)
-    rmid_split[...] = jnp.zeros_like(rmid_split)
-    store_parts(rmid_split, rmid, NPM)
+    low_t_f32[...] = jnp.zeros_like(low_t_f32)
+    rmid_t_split[...] = jnp.zeros_like(rmid_t_split)
 
     def identity(n):
         rows = lax.broadcasted_iota(jnp.int32, (n, n), 0)
         cols = lax.broadcasted_iota(jnp.int32, (n, n), 1)
         return jnp.where(rows == cols, 1.0, 0.0).astype(F32)
 
+    def below(value, rows):
+        return jnp.concatenate([value, jnp.zeros((rows, value.shape[1]), F32)], axis=0)
+
+    def turned(value):
+        unit = identity(value.shape[1]).astype(BF16)
+        return [
+            lax.dot_general(unit, part, NT, preferred_element_type=F32).astype(BF16)
+            for part in parts(value)
+        ]
+
+    store_parts(rmid_split, below(rmid, NPM - NP1), NPM)
+    store_parts(rboth_split, below(rboth, NPL - NP2), NPL)
+    stacked = jnp.concatenate([below(rmid, NPM - NP1), below(rboth, NPL - NP2)], axis=0)
+    stacked_high, stacked_low = turned(stacked)
     for f in range(FACES + 1):
-        matrix = flux_ref[f] if f < FACES else stiff_ref[...]
-        mid_matrix = exact(exact(rmid, matrix), rmid, NT)
-        mid_f32[0:NP1, f * NP1 : (f + 1) * NP1] = mid_matrix
-        lift_f32[:, f * NP1 : (f + 1) * NP1] = exact(matrix, rmid, NT)
-        low_matrix = exact(exact(rlow, mid_matrix), rlow, NT)
-        low_f32[0:NP2, f * NP2 : (f + 1) * NP2] = low_matrix
-    stiff_low = low_matrix
-    diag_mid = jnp.sum(mid_matrix * identity(NP1), axis=1, keepdims=True)
-    diag_low = jnp.sum(low_matrix * identity(NP2), axis=1, keepdims=True)
-    store_parts(mid_split, mid_f32[...], NPM)
-    store_parts(lift_split, lift_f32[...], NP0)
-    store_parts(low_split, low_f32[...], NPL)
-    rmid_t_split[...] = jnp.zeros_like(rmid_t_split)
-    rmid_t_high, rmid_t_low = parts(exact(identity(NP0), rmid, NT))
-    rmid_t_split[pl.ds(0, NP0), 0:NP1] = rmid_t_high
-    rmid_t_split[pl.ds(NP0, NP0), 0:NP1] = rmid_t_low
-    rlow_t = exact(identity(NP1), rlow, NT)
+        high, low = parts(flux_ref[f] if f < FACES else stiff_ref[...])
+        lifted = (
+            jnp.dot(high, stacked_high, preferred_element_type=F32)
+            + jnp.dot(low, stacked_high, preferred_element_type=F32)
+            + jnp.dot(high, stacked_low, preferred_element_type=F32)
+        )
+        lift_f32[:, f * NPM : (f + 1) * NPM] = lifted[:, :NPM]
+        low_t_f32[:, f * NPL : (f + 1) * NPL] = lifted[:, NPM : NPM + NPL]
+    lift = lift_f32[...]
+    store_parts(lift_split, lift, NP0)
+    mid_matrix = product(rmid_split, NPM, *parts(lift))
+    low_matrix = product(rboth_split, NPL, *parts(low_t_f32[...]))
+    store_parts(mid_split, mid_matrix, NPM)
+    store_parts(low_split, low_matrix, NPL)
+    mid_own = mid_matrix[:NP1, FACES * NPM : FACES * NPM + NP1]
+    stiff_low = low_matrix[:NP2, FACES * NPL : FACES * NPL + NP2]
+    diag_mid = jnp.sum(mid_own * identity(NP1), axis=1, keepdims=True)
+    diag_low = jnp.sum(stiff_low * identity(NP2), axis=1, keepdims=True)
+    rmid_t_split[pl.ds(0, NP0), :] = stacked_high[:, :NPM]
+    rmid_t_split[pl.ds(NP0, NP0), :] = stacked_low[:, :NPM]
+    rlow_t_high, rlow_t_low = turned(below(rlow, NPL - NP2))
+    rlow_t = jnp.concatenate([rlow_t_high, rlow_t_low], axis=0)
 
     def second_block(u):
         active = active_of(u)
@@ -283,7 +343,9 @@
         high, low = parts(block)
         rhs = product(rmid_split, NPM, high, low)[:NP1]
         mid_rhs[u] = rhs
-        e3[u + SIDE] = rhs * (DAMPING * active / jac_of(u)) / diag_mid
+        corr = rhs * (DAMPING * active / jac_of(u)) / diag_mid
+        e3[u + SIDE] = corr
+        split_mid(split3, u + SIDE, corr)
 
     over(SIDE, PAIRS - SIDE, second_block)
     finish(second_halo)
@@ -291,36 +353,36 @@
     over_edges(second_block)
     mid_halo = exchange(2, e3)
 
-    def gathered(u, buffer, rows, padding):
-        reach_lane = lax.broadcasted_iota(jnp.int32, (8, LANES), 1)
-        pieces = []
+    def mid_feed(u, buffer, split):
+        around = jnp.concatenate([split[u + j] for j in range(SPAN)], axis=1)
         for f in range(FACES):
-            halves = []
-            for h in range(2):
-                offset = offset_ref[pl.ds(f * ROWS_PER + 2 * u + h, 1), :]
-                reach = jnp.broadcast_to(offset, (8, LANES)) + reach_lane + HALO
-                inner = reach & (LANES - 1)
-                outer = reach >> 7
-                groups = []
-                for g in range(rows // 8):
-                    value = jnp.zeros((8, LANES), F32)
-                    for j in range(2 * HALO // LANES + 1):
-                        b = h + j
-                        source = buffer[
-                            u + b // 2, pl.ds(8 * g, 8), pl.ds((b % 2) * LANES, LANES)
-                        ]
-                        found = jnp.take_along_axis(source, inner, axis=1)
-                        value = jnp.where(outer == j, found, value)
-                    groups.append(value)
-                halves.append(jnp.concatenate(groups, axis=0))
-            pieces.append(jnp.concatenate(halves, axis=1) * weight_of(f, u))
-        pieces.append(jac_of(u) * buffer[u + SIDE])
-        pieces.append(jnp.zeros((padding, PAIR), F32))
-        return parts(jnp.concatenate(pieces, axis=0))
+            if f < MX_FACES:
+                both = jnp.dot(around, pick[u, f], preferred_element_type=F32)
+                value = both[:NPM] + both[NPM:]
+            else:
+                value = lane_gather(u, buffer, f, 0, NP1, NPM - NP1)
+            high, low = parts(value * weight_of(f, u))
+            feed_mid[0, pl.ds(f * NPM, NPM), :] = high
+            feed_mid[1, pl.ds(f * NPM, NPM), :] = low
+        high, low = parts(below(jac_of(u) * buffer[u + SIDE], NPM - NP1))
+        feed_mid[0, pl.ds(FACES * NPM, NPM), :] = high
+        feed_mid[1, pl.ds(FACES * NPM, NPM), :] = low
+        return feed_mid[0], feed_mid[1]
+
+    def low_feed(u, buffer):
+        for f in range(FACES):
+            value = lane_gather(u, buffer, f, 0, NP2, NPL - NP2)
+            high, low = parts(value * weight_of(f, u))
+            feed_coarse[0, pl.ds(f * NPL, NPL), :] = high
+            feed_coarse[1, pl.ds(f * NPL, NPL), :] = low
+        high, low = parts(below(jac_of(u) * buffer[u + SIDE], NPL - NP2))
+        feed_coarse[0, pl.ds(FACES * NPL, NPL), :] = high
+        feed_coarse[1, pl.ds(FACES * NPL, NPL), :] = low
+        return feed_coarse[0], feed_coarse[1]
 
     def mid_block(u):
         active = active_of(u)
-        high, low = gathered(u, e3, NP1, KM - 5 * NP1)
+        high, low = mid_feed(u, e3, split3)
         mid_res = mid_rhs[u] - active * product(mid_split, NPM, high, low)[:NP1]
         rhs = exact(rlow, mid_res)
         low_rhs[u] = rhs
@@ -328,12 +390,14 @@
 
     over(SIDE, PAIRS - SIDE, mid_block)
     finish(mid_halo)
+    for b in halo_blocks:
+        split_mid(split3, b, e3[b])
     over_edges(mid_block)
     low_halo = exchange(3, e4)
 
     def low_block(u):
         active = active_of(u)
-        high, low = gathered(u, e4, NP2, KL - 5 * NP2)
+        high, low = low_feed(u, e4)
         low_res[u] = low_rhs[u] - active * product(low_split, NPL, high, low)[:NP2]
 
     over(SIDE, PAIRS - SIDE, low_block)
@@ -381,25 +445,31 @@
         active = active_of(u)
         both = jnp.dot(corr_split, members(u), preferred_element_type=F32)
         low_total = e4[u + SIDE] + active * (both[:NP2] + both[NPL : NPL + NP2])
-        e5[u + SIDE] = e3[u + SIDE] + exact(rlow_t, low_total)
-
-    over(0, PAIRS, ascend_block)
+        high, low = parts(below(low_total, NPL - NP2))
+        up = jnp.dot(rlow_t, high, preferred_element_type=F32)
+        up = up[:NP1] + up[NP1:] + jnp.dot(rlow_t[:NP1], low, preferred_element_type=F32)
+        total = e3[u + SIDE] + up
+        e5[u + SIDE] = total
+        split_mid(split5, u + SIDE, total)
+
+    over_edges(ascend_block)
     last_halo = exchange(4, e5)
+    over(SIDE, PAIRS - SIDE, ascend_block)
 
     def update_block(u):
-        high, low = parts(
-            jnp.concatenate([e5[u + SIDE], jnp.zeros((NPM - NP1, PAIR), F32)], axis=0)
-        )
+        high, low = split5[u + SIDE, pl.ds(0, NPM), :], split5[u + SIDE, pl.ds(NPM, NPM), :]
         put_wide(upd_ref, u, e2[u + SIDE] + product(rmid_t_split, NP0, high, low))
 
     over(0, PAIRS, update_block)
 
     def residual_block(u):
-        high, low = gathered(u, e5, NP1, KM - 5 * NP1)
+        high, low = mid_feed(u, e5, split5)
         put_wide(res_ref, u, second[u] - active_of(u) * product(lift_split, NP0, high, low))
 
     over(SIDE, PAIRS - SIDE, residual_block)
     finish(last_halo)
+    for b in halo_blocks:
+        split_mid(split5, b, e5[b])
     over_edges(residual_block)
 
 
@@ -436,26 +506,30 @@
             pltpu.VMEM((EXT, NP1, PAIR), F32),
             pltpu.VMEM((EXT, NP2, PAIR), F32),
             pltpu.VMEM((EXT, NP1, PAIR), F32),
-            pltpu.VMEM((EXT, 2 * NP0, PAIR), BF16),
-            pltpu.VMEM((EXT, 2 * NP0, PAIR), BF16),
+            pltpu.VMEM((EXT, 2 * MX_ROWS, PAIR), BF16),
+            pltpu.VMEM((EXT, 2 * MX_ROWS, PAIR), BF16),
             pltpu.VMEM((PAIRS, FACES, SPAN * PAIR, PAIR), BF16),
             pltpu.VMEM((PAIRS, NP0, PAIR), F32),
+            pltpu.VMEM((EXT, 2 * NPM, PAIR), BF16),
+            pltpu.VMEM((EXT, 2 * NPM, PAIR), BF16),
             pltpu.VMEM((PAIRS, NP1, PAIR), F32),
             pltpu.VMEM((PAIRS, NP2, PAIR), F32),
             pltpu.VMEM((PAIRS, NP2, PAIR), F32),
             pltpu.VMEM((KF, PAIR), BF16),
             pltpu.VMEM((KF, PAIR), BF16),
+            pltpu.VMEM((2, KM, PAIR), BF16),
+            pltpu.VMEM((2, KL, PAIR), BF16),
             pltpu.VMEM((NP0, KF), F32),
             pltpu.VMEM((2 * NP0, KF), BF16),
             pltpu.VMEM((2 * NP0, NP0), BF16),
             pltpu.VMEM((2 * NPM, NP0), BF16),
-            pltpu.VMEM((NPM, KM), F32),
+            pltpu.VMEM((2 * NPL, NP0), BF16),
             pltpu.VMEM((2 * NPM, KM), BF16),
             pltpu.VMEM((NP0, KM), F32),
             pltpu.VMEM((2 * NP0, KM), BF16),
-            pltpu.VMEM((NPL, KL), F32),
             pltpu.VMEM((2 * NPL, KL), BF16),
             pltpu.VMEM((2 * NP0, NPM), BF16),
+            pltpu.VMEM((NP0, KL), F32),
             pltpu.VMEM((HLEV, NP2, EC_DEV), F32),
             pltpu.VMEM((HLEV, NP2, EC_DEV), F32),
             pltpu.SemaphoreType.DMA((5, 2)),
@@ -464,7 +538,7 @@
             pltpu.SemaphoreType.DMA((HLEV,)),
         ],
         compiler_params=pltpu.CompilerParams(
-            collective_id=0, has_side_effects=True, vmem_limit_bytes=60 * 1024 * 1024
+            collective_id=0, has_side_effects=True, vmem_limit_bytes=44 * 1024 * 1024
         ),
     )(
         flat(iterate),

time: 91.9 us -> 89.8 us (0.977)
  Pallas kernels: 85.8 us -> 75.6 us
  local copies, waits for them, and re-layouts: 4.66 us -> 12.3 us
    pallas_call x1, Pallas kernels: 85.8 us -> 75.6 us  [on_device(): pl.pallas_call(partial(kernel, n_dom, n_fold), out_shape=(out, out), in_s...]
    unnamed x4 -> x24, local copies, waits for them, and re-layouts: 4.66 us -> 12.3 us
where the time goes in v2:
time: 89.8 us; the launch traced here: 89.2 us
  Pallas kernels  75.6 us (84%)
  local copies, waits for them, and re-layouts  12.3 us (14%)
  between operations  1.31 us (1%)
    pallas_call x1, Pallas kernels, on_device(): pl.pallas_call(partial(kernel, n_dom, n_fold), out_shape=(out, out), in_s...  75.6 us
    unnamed x24, local copies, waits for them, and re-layouts  12.3 us

profile of v2, /device:TPU:1, one launch (start us, length us, event | category | flops | bytes accessed | tf_op | source)
XLA Modules:
  0.0 89.2 jit_solution(7506115802937419569)
XLA Ops:
  1.3 0.0 copy-start
  1.3 1.4 %copy-done = f32[176,1,2048]{2,1,0:T(1,128)S(1)} copy-done((f32[176,1,2048]{2,1,0:T(1,128)S(1)}, f32[176,1,2048]{2,1,0:T(1,128)}, u32[]{:S(2)}) %copy-start) | copy-done | bytes 1441816
  2.6 0.0 copy-start.1
  2.6 1.4 %copy-done.1 = f32[176,1,2048]{2,1,0:T(1,128)S(1)} copy-done((f32[176,1,2048]{2,1,0:T(1,128)S(1)}, f32[176,1,2048]{2,1,0:T(1,128)}, u32[]{:S(2)}) %copy-start.1) | copy-done | bytes 1441816
  4.0 0.0 copy-start.2
  4.0 1.1 %copy-done.2 = f32[4,176,176]{2,1,0:T(8,128)S(1)} copy-done((f32[4,176,176]{2,1,0:T(8,128)S(1)}, f32[4,176,176]{2,1,0:T(8,128)}, u32[]{:S(2)}) %copy-start.2) | copy-done | bytes 495640
  5.1 0.0 copy-start.3
  5.1 0.9 %copy-done.3 = f32[176,176]{1,0:T(8,128)S(1)} copy-done((f32[176,176]{1,0:T(8,128)S(1)}, f32[176,176]{1,0:T(8,128)}, u32[]{:S(2)}) %copy-start.3) | copy-done | bytes 123928
  6.0 0.0 copy-start.4
  6.0 0.9 %copy-done.4 = f32[176,176]{1,0:T(8,128)S(1)} copy-done((f32[176,176]{1,0:T(8,128)S(1)}, f32[176,176]{1,0:T(8,128)}, u32[]{:S(2)}) %copy-start.4) | copy-done | bytes 123928
  7.0 0.0 copy-start.5
  7.0 0.8 copy-done.5
  7.8 0.0 copy-start.6
  7.8 0.8 copy-done.6
  8.5 0.0 copy-start.7
  8.5 0.8 copy-done.7
  9.3 0.0 copy-start.8
  9.3 0.7 copy-done.8
  10.0 0.0 copy-start.9
  10.0 0.7 copy-done.9
  10.7 0.0 copy-start.10
  10.7 0.7 copy-done.10
  11.4 75.6 %shard_map.131 = (f32[2816,128]{1,0:T(8,128)S(1)}, f32[2816,128]{1,0:T(8,128)S(1)}) custom-call(f32[2816,128]{1,0:T(8,128)S(1)} %bitcast.8, f32[2816,128]{1,0:T(8,128)S(1)} %bitcast.9, f32[16,128]{1,0:T(8,128)S(1)} %bitcast.14, f32[64,128]{1,0:T(8,128)S(1)} %bitcast.12, s32[64,128]{1,0:T(8,128)S(1)} %bitcast.13, s32[16,128]{1,0:T(8,128)S(1)} %bitcast.15, ...), custom_call_target="tpu_custom_call" | custom-call | tf_op jit(solution)/shard_map/pallas_call | solution.py:498
  87.0 1.1 %copy.19 = f32[176,1,2048]{2,1,0:T(1,128)} copy(f32[176,1,2048]{2,1,0:T(1,128)S(1)} %bitcast.11) | data formatting | bytes 2883584
  88.1 1.1 %copy.20 = f32[176,1,2048]{2,1,0:T(1,128)} copy(f32[176,1,2048]{2,1,0:T(1,128)S(1)} %bitcast.10) | data formatting | bytes 2883584
Async XLA Ops:
  1.3 1.4 %copy-start = (f32[176,1,2048]{2,1,0:T(1,128)S(1)}, f32[176,1,2048]{2,1,0:T(1,128)}, u32[]{:S(2)}) copy-start(f32[176,1,2048]{2,1,0:T(1,128)} %param.12) | copy-start | bytes 4325380
  2.6 1.4 %copy-start.1 = (f32[176,1,2048]{2,1,0:T(1,128)S(1)}, f32[176,1,2048]{2,1,0:T(1,128)}, u32[]{:S(2)}) copy-start(f32[176,1,2048]{2,1,0:T(1,128)} %param.13) | copy-start | bytes 4325380
  4.0 1.1 %copy-start.2 = (f32[4,176,176]{2,1,0:T(8,128)S(1)}, f32[4,176,176]{2,1,0:T(8,128)}, u32[]{:S(2)}) copy-start(f32[4,176,176]{2,1,0:T(8,128)} %flux_ref.1) | copy-start | bytes 1486852
  5.1 0.9 %copy-start.3 = (f32[176,176]{1,0:T(8,128)S(1)}, f32[176,176]{1,0:T(8,128)}, u32[]{:S(2)}) copy-start(f32[176,176]{1,0:T(8,128)} %stiff_ref.1) | copy-start | bytes 371716
  6.0 0.9 %copy-start.4 = (f32[176,176]{1,0:T(8,128)S(1)}, f32[176,176]{1,0:T(8,128)}, u32[]{:S(2)}) copy-start(f32[176,176]{1,0:T(8,128)} %smoother_ref.1) | copy-start | bytes 371716
  7.0 0.8 copy-start.5
  7.8 0.8 copy-start.6
  8.5 0.8 copy-start.7
  9.3 0.7 copy-start.8
  10.0 0.7 copy-start.9
  10.7 0.7 copy-start.10

commit v3 on v2

--- a/solution.py
+++ b/solution.py
@@ -60,20 +60,31 @@
 def kernel(
     n_dom,
     n_fold,
+    iter_hbm,
+    rhs_hbm,
+    jac_hbm,
+    scale_hbm,
+    offset_hbm,
+    agg_hbm,
+    live_ref,
+    stiff_hbm,
+    flux_hbm,
+    smoother_hbm,
+    rmid_hbm,
+    rlow_hbm,
+    upd_ref,
+    res_ref,
     iter_ref,
     rhs_ref,
     jac_ref,
     scale_ref,
     offset_ref,
     agg_ref,
-    live_ref,
     stiff_ref,
     flux_ref,
     smoother_ref,
     rmid_ref,
     rlow_ref,
-    upd_ref,
-    res_ref,
     e1,
     e2,
     e3,
@@ -87,7 +98,7 @@
     split5,
     mid_rhs,
     low_rhs,
-    low_res,
+    coarse_sum,
     feed_high,
     feed_low,
     feed_mid,
@@ -109,16 +120,37 @@
     recv_sem,
     swap_send,
     swap_recv,
+    load_sem,
 ):
     me = lax.axis_index("dom")
     fold = lax.axis_index("fold")
     right = lax.rem(me + 1, n_dom)
     left = lax.rem(me + n_dom - 1, n_dom)
-    partners = []
-    for height in range(HLEV):
-        step = 2**height
-        bit = (fold // step) % 2
-        partners.append(fold + step - 2 * step * bit)
+    low_bit, high_bit = fold % 2, (fold // 2) % 2
+    flip = fold + 1 - 2 * low_bit
+    across = 2 - 4 * high_bit
+    partners = (flip, fold + across, flip + across)
+
+    loads = [
+        pltpu.make_async_copy(source, target, load_sem.at[i])
+        for i, (source, target) in enumerate(
+            (
+                (iter_hbm, iter_ref),
+                (offset_hbm, offset_ref),
+                (flux_hbm, flux_ref),
+                (stiff_hbm, stiff_ref),
+                (smoother_hbm, smoother_ref),
+                (scale_hbm, scale_ref),
+                (jac_hbm, jac_ref),
+                (rhs_hbm, rhs_ref),
+                (rmid_hbm, rmid_ref),
+                (rlow_hbm, rlow_ref),
+                (agg_hbm, agg_ref),
+            )
+        )
+    ]
+    for load in loads:
+        load.start()
 
     barrier = pltpu.get_barrier_semaphore()
     for other in (left, right):
@@ -155,45 +187,42 @@
         for h in range(2):
             ref[pl.ds(2 * u + h, NP0, stride=ROWS_PER), :] = value[:, h * LANES : (h + 1) * LANES]
 
-    def exchange(k, buffer):
-        to_right = pltpu.make_async_remote_copy(
-            src_ref=buffer.at[pl.ds(PAIRS, SIDE)],
-            dst_ref=buffer.at[pl.ds(0, SIDE)],
-            send_sem=send_sem.at[k, 0],
-            recv_sem=recv_sem.at[k, 0],
-            device_id={"dom": right},
+    pending = []
+
+    def send(k, buffer, side):
+        copy = pltpu.make_async_remote_copy(
+            src_ref=buffer.at[pl.ds(PAIRS if side == 0 else SIDE, SIDE)],
+            dst_ref=buffer.at[pl.ds(0 if side == 0 else SIDE + PAIRS, SIDE)],
+            send_sem=send_sem.at[k, side],
+            recv_sem=recv_sem.at[k, side],
+            device_id={"dom": right if side == 0 else left},
             device_id_type=MESH,
         )
-        to_left = pltpu.make_async_remote_copy(
-            src_ref=buffer.at[pl.ds(SIDE, SIDE)],
-            dst_ref=buffer.at[pl.ds(SIDE + PAIRS, SIDE)],
-            send_sem=send_sem.at[k, 1],
-            recv_sem=recv_sem.at[k, 1],
-            device_id={"dom": left},
-            device_id_type=MESH,
-        )
-        to_right.start()
-        to_left.start()
-        return to_right, to_left
-
-    def finish(copies):
-        for copy in copies:
-            copy.wait()
+        copy.start()
+        pending.append(copy)
+        return copy
 
     def over(first, last, body):
         lax.fori_loop(first, last, lambda i, c: (body(i), c)[1], 0)
 
-    def over_edges(body):
-        lax.fori_loop(
-            0, 2 * SIDE, lambda i, c: (body(i + (i // SIDE) * (PAIRS - 2 * SIDE)), c)[1], 0
-        )
+    def over_left(body):
+        over(0, SIDE, body)
+
+    def over_right(body):
+        over(PAIRS - SIDE, PAIRS, body)
 
     def mask_block(u):
         e1[u + SIDE] = active_of(u) * wide(iter_ref, u)
 
-    over(0, PAIRS, mask_block)
-    pl.semaphore_wait(barrier, 2 + HLEV)
-    first_halo = exchange(0, e1)
+    loads[0].wait()
+    over_left(mask_block)
+    over_right(mask_block)
+    pl.semaphore_wait(barrier, 2 + len(partners))
+    from_left = send(0, e1, 0)
+    from_right = send(0, e1, 1)
+    over(SIDE, PAIRS - SIDE, mask_block)
+    for load in loads[1:]:
+        load.wait()
 
     def split_block(source, target, b):
         store_parts(target.at[b], source[b, pl.ds(0, MX_ROWS), :], MX_ROWS)
@@ -202,11 +231,8 @@
         padded = jnp.concatenate([value, jnp.zeros((NPM - NP1, PAIR), F32)], axis=0)
         store_parts(target.at[b], padded, NPM)
 
-    halo_blocks = (*range(SIDE), *range(SIDE + PAIRS, EXT))
-
-    def split_halo(source, target):
-        for b in halo_blocks:
-            split_block(source, target, b)
+    left_halo = tuple(range(SIDE))
+    right_halo = tuple(range(SIDE + PAIRS, EXT))
 
     over(SIDE, SIDE + PAIRS, lambda b: split_block(e1, split1, b))
 
@@ -281,10 +307,6 @@
         store_parts(split2.at[u + SIDE], block[:MX_ROWS], MX_ROWS)
 
     over(SIDE, PAIRS - SIDE, smooth_block)
-    finish(first_halo)
-    split_halo(e1, split1)
-    over_edges(smooth_block)
-    second_halo = exchange(1, e2)
 
     rmid = rmid_ref[...]
     rlow = rlow_ref[...]
@@ -336,6 +358,17 @@
     rlow_t_high, rlow_t_low = turned(below(rlow, NPL - NP2))
     rlow_t = jnp.concatenate([rlow_t_high, rlow_t_low], axis=0)
 
+    from_left.wait_recv()
+    for b in left_halo:
+        split_block(e1, split1, b)
+    over_left(smooth_block)
+    to_left = send(1, e2, 1)
+    from_right.wait_recv()
+    for b in right_halo:
+        split_block(e1, split1, b)
+    over_right(smooth_block)
+    to_right = send(1, e2, 0)
+
     def second_block(u):
         active = active_of(u)
         block = active * (wide(rhs_ref, u) - fine_apply(u, e2, split2, False))
@@ -348,10 +381,16 @@
         split_mid(split3, u + SIDE, corr)
 
     over(SIDE, PAIRS - SIDE, second_block)
-    finish(second_halo)
-    split_halo(e2, split2)
-    over_edges(second_block)
-    mid_halo = exchange(2, e3)
+    to_left.wait_recv()
+    for b in right_halo:
+        split_block(e2, split2, b)
+    over_right(second_block)
+    mid_right = send(2, e3, 0)
+    to_right.wait_recv()
+    for b in left_halo:
+        split_block(e2, split2, b)
+    over_left(second_block)
+    mid_left = send(2, e3, 1)
 
     def mid_feed(u, buffer, split):
         around = jnp.concatenate([split[u + j] for j in range(SPAN)], axis=1)
@@ -389,57 +428,66 @@
         e4[u + SIDE] = rhs * (DAMPING * active / jac_of(u)) / diag_low
 
     over(SIDE, PAIRS - SIDE, mid_block)
-    finish(mid_halo)
-    for b in halo_blocks:
+    mid_right.wait_recv()
+    for b in left_halo:
         split_mid(split3, b, e3[b])
-    over_edges(mid_block)
-    low_halo = exchange(3, e4)
+    over_left(mid_block)
+    low_left = send(3, e4, 1)
+    mid_left.wait_recv()
+    for b in right_halo:
+        split_mid(split3, b, e3[b])
+    over_right(mid_block)
+    low_right = send(3, e4, 0)
+
+    def members(u):
+        rows = lax.broadcasted_iota(jnp.int32, (EC_DEV, PAIR), 0)
+        return jnp.where(rows == row_of(agg_ref, 0, u), 1.0, 0.0).astype(BF16)
+
+    coarse_sum[...] = jnp.zeros_like(coarse_sum)
 
     def low_block(u):
         active = active_of(u)
         high, low = low_feed(u, e4)
-        low_res[u] = low_rhs[u] - active * product(low_split, NPL, high, low)[:NP2]
+        low_res = low_rhs[u] - active * product(low_split, NPL, high, low)[:NP2]
+        both = lax.dot_general(
+            jnp.concatenate(parts(below(low_res, NPL - NP2)), axis=0),
+            members(u),
+            NT,
+            preferred_element_type=F32,
+        )
+        coarse_sum[...] += both[:NP2] + both[NPL : NPL + NP2]
 
     over(SIDE, PAIRS - SIDE, low_block)
-    finish(low_halo)
-    over_edges(low_block)
-
-    def members(u):
-        rows = lax.broadcasted_iota(jnp.int32, (EC_DEV, PAIR), 0)
-        return jnp.where(rows == row_of(agg_ref, 0, u), 1.0, 0.0).astype(BF16)
-
-    def coarse_block(u, total):
-        high, low = parts(
-            jnp.concatenate([low_res[u], jnp.zeros((NPL - NP2, PAIR), F32)], axis=0)
-        )
-        both = lax.dot_general(
-            jnp.concatenate([high, low], axis=0), members(u), NT, preferred_element_type=F32
-        )
-        return total + both[:NP2] + both[NPL : NPL + NP2]
-
-    coarse = lax.fori_loop(0, PAIRS, coarse_block, jnp.zeros((NP2, EC_DEV), F32))
-    sections = []
-    for height in range(HLEV):
-        scaled = coarse / diag_low
-        sections.append(scaled * (DAMPING / (AGG * 2**height)))
-        residue = coarse - DAMPING * exact(stiff_low, scaled)
-        swap_out[height] = residue
-        copy = pltpu.make_async_remote_copy(
-            src_ref=swap_out.at[height],
-            dst_ref=swap_in.at[height],
-            send_sem=swap_send.at[height],
-            recv_sem=swap_recv.at[height],
-            device_id={"fold": partners[height]},
+    low_left.wait_recv()
+    over_right(low_block)
+    low_right.wait_recv()
+    over_left(low_block)
+
+    def smoothed_away(value):
+        return value - DAMPING * exact(stiff_low, value / diag_low)
+
+    coarse = coarse_sum[...]
+    residue = smoothed_away(coarse)
+    swap_out[...] = residue
+    swaps = [
+        pltpu.make_async_remote_copy(
+            src_ref=swap_out,
+            dst_ref=swap_in.at[i],
+            send_sem=swap_send.at[i],
+            recv_sem=swap_recv.at[i],
+            device_id={"fold": other},
             device_id_type=MESH,
         )
-        copy.start()
-        copy.wait()
-        coarse = residue + swap_in[height]
-    corr = coarse / diag_low * (DAMPING / (AGG * 2**HLEV))
-    for height in reversed(range(HLEV)):
-        corr = sections[height] + corr
-    corr_high, corr_low = parts(jnp.concatenate([corr, jnp.zeros((NPL - NP2, EC_DEV), F32)], axis=0))
-    corr_split = jnp.concatenate([corr_high, corr_low], axis=0)
+        for i, other in enumerate(partners)
+    ]
+    for swap in swaps:
+        swap.start()
+    for swap in swaps:
+        swap.wait_recv()
+    pair_sum = residue + swap_in[0]
+    top = smoothed_away(pair_sum + (swap_in[1] + swap_in[2]))
+    corr = (DAMPING / AGG) * (coarse + 0.5 * pair_sum + 0.25 * top) / diag_low
+    corr_split = jnp.concatenate(parts(below(corr, NPL - NP2)), axis=0)
 
     def ascend_block(u):
         active = active_of(u)
@@ -452,25 +500,37 @@
         e5[u + SIDE] = total
         split_mid(split5, u + SIDE, total)
 
-    over_edges(ascend_block)
-    last_halo = exchange(4, e5)
-    over(SIDE, PAIRS - SIDE, ascend_block)
-
     def update_block(u):
         high, low = split5[u + SIDE, pl.ds(0, NPM), :], split5[u + SIDE, pl.ds(NPM, NPM), :]
         put_wide(upd_ref, u, e2[u + SIDE] + product(rmid_t_split, NP0, high, low))
 
-    over(0, PAIRS, update_block)
+    def ascend_both(u):
+        ascend_block(u)
+        update_block(u)
+
+    over_left(ascend_block)
+    last_left = send(4, e5, 1)
+    over_right(ascend_block)
+    last_right = send(4, e5, 0)
+    over(SIDE, PAIRS - SIDE, ascend_both)
+    over_left(update_block)
+    over_right(update_block)
 
     def residual_block(u):
         high, low = mid_feed(u, e5, split5)
         put_wide(res_ref, u, second[u] - active_of(u) * product(lift_split, NP0, high, low))
 
     over(SIDE, PAIRS - SIDE, residual_block)
-    finish(last_halo)
-    for b in halo_blocks:
+    last_left.wait_recv()
+    for b in right_halo:
         split_mid(split5, b, e5[b])
-    over_edges(residual_block)
+    over_right(residual_block)
+    last_right.wait_recv()
+    for b in left_halo:
+        split_mid(split5, b, e5[b])
+    over_left(residual_block)
+    for copy in (*pending, *swaps):
+        copy.wait_send()
 
 
 def on_device(
@@ -490,17 +550,32 @@
     restrict_low,
 ):
     def flat(array):
-        return array.reshape(-1, LANES)
+        return held(array.reshape(-1, LANES))
+
+    def held(array):
+        return pltpu.with_memory_space_constraint(array, pltpu.HBM)
 
     vmem = pl.BlockSpec(memory_space=pltpu.VMEM)
+    hbm = pl.BlockSpec(memory_space=pltpu.HBM)
     smem = pl.BlockSpec(memory_space=pltpu.SMEM)
     out = jax.ShapeDtypeStruct((NP0 * ROWS_PER, LANES), F32)
     updated, residual = pl.pallas_call(
         partial(kernel, n_dom, n_fold),
         out_shape=(out, out),
-        in_specs=[vmem] * 6 + [smem] + [vmem] * 5,
+        in_specs=[hbm] * 6 + [smem] + [hbm] * 5,
         out_specs=(vmem, vmem),
         scratch_shapes=[
+            pltpu.VMEM((NP0 * ROWS_PER, LANES), F32),
+            pltpu.VMEM((NP0 * ROWS_PER, LANES), F32),
+            pltpu.VMEM((ROWS_PER, LANES), F32),
+            pltpu.VMEM((FACES * ROWS_PER, LANES), F32),
+            pltpu.VMEM((FACES * ROWS_PER, LANES), jnp.int32),
+            pltpu.VMEM((ROWS_PER, LANES), jnp.int32),
+            pltpu.VMEM((NP0, NP0), F32),
+            pltpu.VMEM((FACES, NP0, NP0), F32),
+            pltpu.VMEM((NP0, NP0), F32),
+            pltpu.VMEM((NP1, NP0), F32),
+            pltpu.VMEM((NP2, NP1), F32),
             pltpu.VMEM((EXT, NP0, PAIR), F32),
             pltpu.VMEM((EXT, NP0, PAIR), F32),
             pltpu.VMEM((EXT, NP1, PAIR), F32),
@@ -514,7 +589,7 @@
             pltpu.VMEM((EXT, 2 * NPM, PAIR), BF16),
             pltpu.VMEM((PAIRS, NP1, PAIR), F32),
             pltpu.VMEM((PAIRS, NP2, PAIR), F32),
-            pltpu.VMEM((PAIRS, NP2, PAIR), F32),
+            pltpu.VMEM((NP2, EC_DEV), F32),
             pltpu.VMEM((KF, PAIR), BF16),
             pltpu.VMEM((KF, PAIR), BF16),
             pltpu.VMEM((2, KM, PAIR), BF16),
@@ -530,12 +605,13 @@
             pltpu.VMEM((2 * NPL, KL), BF16),
             pltpu.VMEM((2 * NP0, NPM), BF16),
             pltpu.VMEM((NP0, KL), F32),
-            pltpu.VMEM((HLEV, NP2, EC_DEV), F32),
-            pltpu.VMEM((HLEV, NP2, EC_DEV), F32),
+            pltpu.VMEM((NP2, EC_DEV), F32),
+            pltpu.VMEM((3, NP2, EC_DEV), F32),
             pltpu.SemaphoreType.DMA((5, 2)),
             pltpu.SemaphoreType.DMA((5, 2)),
-            pltpu.SemaphoreType.DMA((HLEV,)),
-            pltpu.SemaphoreType.DMA((HLEV,)),
+            pltpu.SemaphoreType.DMA((3,)),
+            pltpu.SemaphoreType.DMA((3,)),
+            pltpu.SemaphoreType.DMA((11,)),
         ],
         compiler_params=pltpu.CompilerParams(
             collective_id=0, has_side_effects=True, vmem_limit_bytes=44 * 1024 * 1024
@@ -548,11 +624,11 @@
         flat(face_offset),
         flat(agglomerate),
         live_count,
-        stiff_fine,
-        flux_fine,
-        smoother,
-        restrict_mid,
-        restrict_low,
+        held(stiff_fine),
+        held(flux_fine),
+        held(smoother),
+        held(restrict_mid),
+        held(restrict_low),
     )
     return updated.reshape(iterate.shape), residual.reshape(iterate.shape)
 

time: 89.8 us -> 71.3 us (0.79)
  local copies, waits for them, and re-layouts: 12.3 us -> 2.2 us
  Pallas kernels: 75.6 us -> 67.7 us
    unnamed x24 -> x2, local copies, waits for them, and re-layouts: 12.3 us -> 2.2 us
    pallas_call x1, Pallas kernels: 75.6 us -> 67.7 us  [on_device(): pl.pallas_call(partial(kernel, n_dom, n_fold), out_shape=(out, out), in_s...]
where the time goes in v3:
time: 71.3 us; the launch traced here: 71.2 us
  Pallas kernels  67.7 us (95%)
  local copies, waits for them, and re-layouts  2.2 us (3%)
  between operations  1.29 us (2%)
    pallas_call x1, Pallas kernels, on_device(): pl.pallas_call(partial(kernel, n_dom, n_fold), out_shape=(out, out), in_s...  67.7 us
    unnamed x2, local copies, waits for them, and re-layouts  2.2 us

profile of v3, /device:TPU:1, one launch (start us, length us, event | category | flops | bytes accessed | tf_op | source)
XLA Modules:
  0.0 71.2 jit_solution(4844065251466394058)
XLA Ops:
  1.3 67.7 %shard_map.131 = (f32[2816,128]{1,0:T(8,128)S(1)}, f32[2816,128]{1,0:T(8,128)S(1)}) custom-call(f32[2816,128]{1,0:T(8,128)} %bitcast.10, f32[2816,128]{1,0:T(8,128)} %bitcast.11, f32[16,128]{1,0:T(8,128)} %bitcast.14, f32[64,128]{1,0:T(8,128)} %bitcast.12, s32[64,128]{1,0:T(8,128)} %bitcast.13, s32[16,128]{1,0:T(8,128)} %bitcast.15, ...), custom_call_target="tpu_custom_call" | custom-call | tf_op jit(solution)/shard_map/pallas_call | solution.py:562
  69.0 1.1 %copy.19 = f32[176,1,2048]{2,1,0:T(1,128)} copy(f32[176,1,2048]{2,1,0:T(1,128)S(1)} %bitcast.9) | data formatting | bytes 2883584
  70.1 1.1 %copy.20 = f32[176,1,2048]{2,1,0:T(1,128)} copy(f32[176,1,2048]{2,1,0:T(1,128)S(1)} %bitcast.8) | data formatting | bytes 2883584

commit v4 on v3

--- a/solution.py
+++ b/solution.py
@@ -113,6 +113,7 @@
     lift_split,
     low_split,
     rmid_t_split,
+    rlow_split,
     low_t_f32,
     swap_out,
     swap_in,
@@ -203,7 +204,19 @@
         return copy
 
     def over(first, last, body):
-        lax.fori_loop(first, last, lambda i, c: (body(i), c)[1], 0)
+        def both(i, carry):
+            body(first + 2 * i, 0)
+            body(first + 2 * i + 1, 1)
+            return carry
+
+        lax.fori_loop(0, (last - first) // 2, both, 0)
+
+    def over_one(first, last, body):
+        def one(i, carry):
+            body(i, 0)
+            return carry
+
+        lax.fori_loop(first, last, one, 0)
 
     def over_left(body):
         over(0, SIDE, body)
@@ -211,7 +224,7 @@
     def over_right(body):
         over(PAIRS - SIDE, PAIRS, body)
 
-    def mask_block(u):
+    def mask_block(u, slot):
         e1[u + SIDE] = active_of(u) * wide(iter_ref, u)
 
     loads[0].wait()
@@ -234,7 +247,7 @@
     left_halo = tuple(range(SIDE))
     right_halo = tuple(range(SIDE + PAIRS, EXT))
 
-    over(SIDE, SIDE + PAIRS, lambda b: split_block(e1, split1, b))
+    over(SIDE, SIDE + PAIRS, lambda b, slot: split_block(e1, split1, b))
 
     fine_f32[...] = jnp.zeros_like(fine_f32)
     for f in range(FACES):
@@ -278,7 +291,7 @@
             halves.append(jnp.concatenate(groups, axis=0))
         return jnp.concatenate(halves, axis=1)
 
-    def fine_apply(u, source, split, build):
+    def fine_apply(u, slot, source, split, build):
         around = jnp.concatenate([split[u + j] for j in range(SPAN)], axis=1)
         for f in range(FACES):
             if build:
@@ -286,27 +299,27 @@
             weight = weight_of(f, u)
             both = jnp.dot(around, pick[u, f], preferred_element_type=F32)
             high, low = parts((both[:MX_ROWS] + both[MX_ROWS:]) * weight)
-            feed_high[pl.ds(f * NP0, MX_ROWS), :] = high
-            feed_low[pl.ds(f * NP0, MX_ROWS), :] = low
+            feed_high[slot, pl.ds(f * NP0, MX_ROWS), :] = high
+            feed_low[slot, pl.ds(f * NP0, MX_ROWS), :] = low
             rest = lane_gather(u, source, f, MX_ROWS, NP0 - MX_ROWS)
             high, low = parts(rest * weight)
-            feed_high[pl.ds(f * NP0 + MX_ROWS, NP0 - MX_ROWS), :] = high
-            feed_low[pl.ds(f * NP0 + MX_ROWS, NP0 - MX_ROWS), :] = low
+            feed_high[slot, pl.ds(f * NP0 + MX_ROWS, NP0 - MX_ROWS), :] = high
+            feed_low[slot, pl.ds(f * NP0 + MX_ROWS, NP0 - MX_ROWS), :] = low
         high, low = parts(jac_of(u) * source[u + SIDE])
-        feed_high[pl.ds(FACES * NP0, NP0), :] = high
-        feed_low[pl.ds(FACES * NP0, NP0), :] = low
-        return product(fine_split, NP0, feed_high[...], feed_low[...])
-
-    def smooth_block(u):
+        feed_high[slot, pl.ds(FACES * NP0, NP0), :] = high
+        feed_low[slot, pl.ds(FACES * NP0, NP0), :] = low
+        return product(fine_split, NP0, feed_high[slot], feed_low[slot])
+
+    def smooth_block(u, slot):
         active = active_of(u)
-        first_res = active * (wide(rhs_ref, u) - fine_apply(u, e1, split1, True))
+        first_res = active * (wide(rhs_ref, u) - fine_apply(u, slot, e1, split1, True))
         high, low = parts(first_res)
         update = product(smooth_split, NP0, high, low)
         block = e1[u + SIDE] + update * (active / jac_of(u))
         e2[u + SIDE] = block
         store_parts(split2.at[u + SIDE], block[:MX_ROWS], MX_ROWS)
 
-    over(SIDE, PAIRS - SIDE, smooth_block)
+    over_one(SIDE, PAIRS - SIDE, smooth_block)
 
     rmid = rmid_ref[...]
     rlow = rlow_ref[...]
@@ -355,23 +368,25 @@
     diag_low = jnp.sum(stiff_low * identity(NP2), axis=1, keepdims=True)
     rmid_t_split[pl.ds(0, NP0), :] = stacked_high[:, :NPM]
     rmid_t_split[pl.ds(NP0, NP0), :] = stacked_low[:, :NPM]
+    rlow_wide = jnp.concatenate([rlow, jnp.zeros((NP2, NPM - NP1), F32)], axis=1)
+    store_parts(rlow_split, below(rlow_wide, NPL - NP2), NPL)
     rlow_t_high, rlow_t_low = turned(below(rlow, NPL - NP2))
     rlow_t = jnp.concatenate([rlow_t_high, rlow_t_low], axis=0)
 
     from_left.wait_recv()
     for b in left_halo:
         split_block(e1, split1, b)
-    over_left(smooth_block)
+    over_one(0, SIDE, smooth_block)
     to_left = send(1, e2, 1)
     from_right.wait_recv()
     for b in right_halo:
         split_block(e1, split1, b)
-    over_right(smooth_block)
+    over_one(PAIRS - SIDE, PAIRS, smooth_block)
     to_right = send(1, e2, 0)
 
-    def second_block(u):
+    def second_block(u, slot):
         active = active_of(u)
-        block = active * (wide(rhs_ref, u) - fine_apply(u, e2, split2, False))
+        block = active * (wide(rhs_ref, u) - fine_apply(u, slot, e2, split2, False))
         second[u] = block
         high, low = parts(block)
         rhs = product(rmid_split, NPM, high, low)[:NP1]
@@ -380,19 +395,19 @@
         e3[u + SIDE] = corr
         split_mid(split3, u + SIDE, corr)
 
-    over(SIDE, PAIRS - SIDE, second_block)
+    over_one(SIDE, PAIRS - SIDE, second_block)
     to_left.wait_recv()
     for b in right_halo:
         split_block(e2, split2, b)
-    over_right(second_block)
+    over_one(PAIRS - SIDE, PAIRS, second_block)
     mid_right = send(2, e3, 0)
     to_right.wait_recv()
     for b in left_halo:
         split_block(e2, split2, b)
-    over_left(second_block)
+    over_one(0, SIDE, second_block)
     mid_left = send(2, e3, 1)
 
-    def mid_feed(u, buffer, split):
+    def mid_feed(u, slot, buffer, split):
         around = jnp.concatenate([split[u + j] for j in range(SPAN)], axis=1)
         for f in range(FACES):
             if f < MX_FACES:
@@ -401,29 +416,30 @@
             else:
                 value = lane_gather(u, buffer, f, 0, NP1, NPM - NP1)
             high, low = parts(value * weight_of(f, u))
-            feed_mid[0, pl.ds(f * NPM, NPM), :] = high
-            feed_mid[1, pl.ds(f * NPM, NPM), :] = low
+            feed_mid[slot, 0, pl.ds(f * NPM, NPM), :] = high
+            feed_mid[slot, 1, pl.ds(f * NPM, NPM), :] = low
         high, low = parts(below(jac_of(u) * buffer[u + SIDE], NPM - NP1))
-        feed_mid[0, pl.ds(FACES * NPM, NPM), :] = high
-        feed_mid[1, pl.ds(FACES * NPM, NPM), :] = low
-        return feed_mid[0], feed_mid[1]
-
-    def low_feed(u, buffer):
+        feed_mid[slot, 0, pl.ds(FACES * NPM, NPM), :] = high
+        feed_mid[slot, 1, pl.ds(FACES * NPM, NPM), :] = low
+        return feed_mid[slot, 0], feed_mid[slot, 1]
+
+    def low_feed(u, slot, buffer):
         for f in range(FACES):
             value = lane_gather(u, buffer, f, 0, NP2, NPL - NP2)
             high, low = parts(value * weight_of(f, u))
-            feed_coarse[0, pl.ds(f * NPL, NPL), :] = high
-            feed_coarse[1, pl.ds(f * NPL, NPL), :] = low
+            feed_coarse[slot, 0, pl.ds(f * NPL, NPL), :] = high
+            feed_coarse[slot, 1, pl.ds(f * NPL, NPL), :] = low
         high, low = parts(below(jac_of(u) * buffer[u + SIDE], NPL - NP2))
-        feed_coarse[0, pl.ds(FACES * NPL, NPL), :] = high
-        feed_coarse[1, pl.ds(FACES * NPL, NPL), :] = low
-        return feed_coarse[0], feed_coarse[1]
-
-    def mid_block(u):
+        feed_coarse[slot, 0, pl.ds(FACES * NPL, NPL), :] = high
+        feed_coarse[slot, 1, pl.ds(FACES * NPL, NPL), :] = low
+        return feed_coarse[slot, 0], feed_coarse[slot, 1]
+
+    def mid_block(u, slot):
         active = active_of(u)
-        high, low = mid_feed(u, e3, split3)
+        high, low = mid_feed(u, slot, e3, split3)
         mid_res = mid_rhs[u] - active * product(mid_split, NPM, high, low)[:NP1]
-        rhs = exact(rlow, mid_res)
+        high, low = parts(below(mid_res, NPM - NP1))
+        rhs = product(rlow_split, NPL, high, low)[:NP2]
         low_rhs[u] = rhs
         e4[u + SIDE] = rhs * (DAMPING * active / jac_of(u)) / diag_low
 
@@ -445,9 +461,9 @@
 
     coarse_sum[...] = jnp.zeros_like(coarse_sum)
 
-    def low_block(u):
+    def low_block(u, slot):
         active = active_of(u)
-        high, low = low_feed(u, e4)
+        high, low = low_feed(u, slot, e4)
         low_res = low_rhs[u] - active * product(low_split, NPL, high, low)[:NP2]
         both = lax.dot_general(
             jnp.concatenate(parts(below(low_res, NPL - NP2)), axis=0),
@@ -489,7 +505,7 @@
     corr = (DAMPING / AGG) * (coarse + 0.5 * pair_sum + 0.25 * top) / diag_low
     corr_split = jnp.concatenate(parts(below(corr, NPL - NP2)), axis=0)
 
-    def ascend_block(u):
+    def ascend_block(u, slot):
         active = active_of(u)
         both = jnp.dot(corr_split, members(u), preferred_element_type=F32)
         low_total = e4[u + SIDE] + active * (both[:NP2] + both[NPL : NPL + NP2])
@@ -500,13 +516,13 @@
         e5[u + SIDE] = total
         split_mid(split5, u + SIDE, total)
 
-    def update_block(u):
+    def update_block(u, slot):
         high, low = split5[u + SIDE, pl.ds(0, NPM), :], split5[u + SIDE, pl.ds(NPM, NPM), :]
         put_wide(upd_ref, u, e2[u + SIDE] + product(rmid_t_split, NP0, high, low))
 
-    def ascend_both(u):
-        ascend_block(u)
-        update_block(u)
+    def ascend_both(u, slot):
+        ascend_block(u, slot)
+        update_block(u, slot)
 
     over_left(ascend_block)
     last_left = send(4, e5, 1)
@@ -516,8 +532,8 @@
     over_left(update_block)
     over_right(update_block)
 
-    def residual_block(u):
-        high, low = mid_feed(u, e5, split5)
+    def residual_block(u, slot):
+        high, low = mid_feed(u, slot, e5, split5)
         put_wide(res_ref, u, second[u] - active_of(u) * product(lift_split, NP0, high, low))
 
     over(SIDE, PAIRS - SIDE, residual_block)
@@ -590,10 +606,10 @@
             pltpu.VMEM((PAIRS, NP1, PAIR), F32),
             pltpu.VMEM((PAIRS, NP2, PAIR), F32),
             pltpu.VMEM((NP2, EC_DEV), F32),
-            pltpu.VMEM((KF, PAIR), BF16),
-            pltpu.VMEM((KF, PAIR), BF16),
-            pltpu.VMEM((2, KM, PAIR), BF16),
-            pltpu.VMEM((2, KL, PAIR), BF16),
+            pltpu.VMEM((2, KF, PAIR), BF16),
+            pltpu.VMEM((2, KF, PAIR), BF16),
+            pltpu.VMEM((2, 2, KM, PAIR), BF16),
+            pltpu.VMEM((2, 2, KL, PAIR), BF16),
             pltpu.VMEM((NP0, KF), F32),
             pltpu.VMEM((2 * NP0, KF), BF16),
             pltpu.VMEM((2 * NP0, NP0), BF16),
@@ -604,6 +620,7 @@
             pltpu.VMEM((2 * NP0, KM), BF16),
             pltpu.VMEM((2 * NPL, KL), BF16),
             pltpu.VMEM((2 * NP0, NPM), BF16),
+            pltpu.VMEM((2 * NPL, NPM), BF16),
             pltpu.VMEM((NP0, KL), F32),
             pltpu.VMEM((NP2, EC_DEV), F32),
             pltpu.VMEM((3, NP2, EC_DEV), F32),
@@ -614,7 +631,7 @@
             pltpu.SemaphoreType.DMA((11,)),
         ],
         compiler_params=pltpu.CompilerParams(
-            collective_id=0, has_side_effects=True, vmem_limit_bytes=44 * 1024 * 1024
+            collective_id=0, has_side_effects=True, vmem_limit_bytes=48 * 1024 * 1024
         ),
     )(
         flat(iterate),

time: 71.3 us -> 68 us (0.954)
  Pallas kernels: 67.7 us -> 64.4 us
    pallas_call x1, Pallas kernels: 67.7 us -> 64.4 us  [on_device(): pl.pallas_call(partial(kernel, n_dom, n_fold), out_shape=(out, out), in_s...]
where the time goes in v4:
time: 68 us; the launch traced here: 67.9 us
  Pallas kernels  64.4 us (95%)
  local copies, waits for them, and re-layouts  2.2 us (3%)
  between operations  1.29 us (2%)
    pallas_call x1, Pallas kernels, on_device(): pl.pallas_call(partial(kernel, n_dom, n_fold), out_shape=(out, out), in_s...  64.4 us
    unnamed x2, local copies, waits for them, and re-layouts  2.2 us

profile of v4, /device:TPU:1, one launch (start us, length us, event | category | flops | bytes accessed | tf_op | source)
XLA Modules:
  0.0 67.9 jit_solution(6325700834780354445)
XLA Ops:
  1.3 64.4 %shard_map.131 = (f32[2816,128]{1,0:T(8,128)S(1)}, f32[2816,128]{1,0:T(8,128)S(1)}) custom-call(f32[2816,128]{1,0:T(8,128)} %bitcast.10, f32[2816,128]{1,0:T(8,128)} %bitcast.11, f32[16,128]{1,0:T(8,128)} %bitcast.14, f32[64,128]{1,0:T(8,128)} %bitcast.12, s32[64,128]{1,0:T(8,128)} %bitcast.13, s32[16,128]{1,0:T(8,128)} %bitcast.15, ...), custom_call_target="tpu_custom_call" | custom-call | tf_op jit(solution)/shard_map/pallas_call | solution.py:578
  65.7 1.1 %copy.19 = f32[176,1,2048]{2,1,0:T(1,128)} copy(f32[176,1,2048]{2,1,0:T(1,128)S(1)} %bitcast.9) | data formatting | bytes 2883584
  66.8 1.1 %copy.20 = f32[176,1,2048]{2,1,0:T(1,128)} copy(f32[176,1,2048]{2,1,0:T(1,128)S(1)} %bitcast.8) | data formatting | bytes 2883584

commit v5 on v4

--- a/solution.py
+++ b/solution.py
@@ -150,8 +150,7 @@
             )
         )
     ]
-    for load in loads:
-        load.start()
+    loads[0].start()
 
     barrier = pltpu.get_barrier_semaphore()
     for other in (left, right):
@@ -228,6 +227,8 @@
         e1[u + SIDE] = active_of(u) * wide(iter_ref, u)
 
     loads[0].wait()
+    for load in loads[1:]:
+        load.start()
     over_left(mask_block)
     over_right(mask_block)
     pl.semaphore_wait(barrier, 2 + len(partners))
@@ -498,21 +499,27 @@
     ]
     for swap in swaps:
         swap.start()
+
+    def up_from_low(value):
+        high, low = parts(below(value, NPL - NP2))
+        both = jnp.dot(rlow_t, high, preferred_element_type=F32)
+        return both[:NP1] + both[NP1:] + jnp.dot(rlow_t[:NP1], low, preferred_element_type=F32)
+
+    def own_block(u, slot):
+        e5[u + SIDE] = e3[u + SIDE] + up_from_low(e4[u + SIDE])
+
+    over(0, PAIRS, own_block)
     for swap in swaps:
         swap.wait_recv()
     pair_sum = residue + swap_in[0]
     top = smoothed_away(pair_sum + (swap_in[1] + swap_in[2]))
     corr = (DAMPING / AGG) * (coarse + 0.5 * pair_sum + 0.25 * top) / diag_low
-    corr_split = jnp.concatenate(parts(below(corr, NPL - NP2)), axis=0)
+    corr_split = jnp.concatenate(parts(below(up_from_low(corr), NPM - NP1)), axis=0)
 
     def ascend_block(u, slot):
         active = active_of(u)
         both = jnp.dot(corr_split, members(u), preferred_element_type=F32)
-        low_total = e4[u + SIDE] + active * (both[:NP2] + both[NPL : NPL + NP2])
-        high, low = parts(below(low_total, NPL - NP2))
-        up = jnp.dot(rlow_t, high, preferred_element_type=F32)
-        up = up[:NP1] + up[NP1:] + jnp.dot(rlow_t[:NP1], low, preferred_element_type=F32)
-        total = e3[u + SIDE] + up
+        total = e5[u + SIDE] + active * (both[:NP1] + both[NPM : NPM + NP1])
         e5[u + SIDE] = total
         split_mid(split5, u + SIDE, total)
 

time: 68 us -> 68 us (level)
  no operation moved by 1% of the time
where the time goes in v5:
time: 68 us; the launch traced here: 67.8 us
  Pallas kernels  64.3 us (95%)
  local copies, waits for them, and re-layouts  2.2 us (3%)
  between operations  1.29 us (2%)
    pallas_call x1, Pallas kernels, on_device(): pl.pallas_call(partial(kernel, n_dom, n_fold), out_shape=(out, out), in_s...  64.3 us
    unnamed x2, local copies, waits for them, and re-layouts  2.2 us

profile of v5, /device:TPU:1, one launch (start us, length us, event | category | flops | bytes accessed | tf_op | source)
XLA Modules:
  0.0 67.8 jit_solution(2202437239203828546)
XLA Ops:
  1.3 64.3 %shard_map.131 = (f32[2816,128]{1,0:T(8,128)S(1)}, f32[2816,128]{1,0:T(8,128)S(1)}) custom-call(f32[2816,128]{1,0:T(8,128)} %bitcast.10, f32[2816,128]{1,0:T(8,128)} %bitcast.11, f32[16,128]{1,0:T(8,128)} %bitcast.14, f32[64,128]{1,0:T(8,128)} %bitcast.12, s32[64,128]{1,0:T(8,128)} %bitcast.13, s32[16,128]{1,0:T(8,128)} %bitcast.15, ...), custom_call_target="tpu_custom_call" | custom-call | tf_op jit(solution)/shard_map/pallas_call | solution.py:585
  65.6 1.1 %copy.19 = f32[176,1,2048]{2,1,0:T(1,128)} copy(f32[176,1,2048]{2,1,0:T(1,128)S(1)} %bitcast.9) | data formatting | bytes 2883584
  66.7 1.1 %copy.20 = f32[176,1,2048]{2,1,0:T(1,128)} copy(f32[176,1,2048]{2,1,0:T(1,128)S(1)} %bitcast.8) | data formatting | bytes 2883584
